TPU v7x, 128 devices: a whole 4x4x4 slice. The times are simulated.
128 devices in a mesh: dp: 8 (over z, core), expert: 16 (over y, x).
Axes of the slice: x: 4, y: 4, z: 4, core: 2. Of those that a mesh axis runs over, the one named last changes fastest.
Arguments:
- inputs: bfloat16 [16384, 2048], P(('dp', 'expert')), may hold values from -6 to 6
- out_grad: bfloat16 [16384, 2048], P(('dp', 'expert')), may hold values from -6 to 6
- combine: float32 [16384, 8], P(('dp', 'expert')), may hold values from 0 to 1, as said below
- routes: int32 [16384, 8], P(('dp', 'expert')), may hold values from 0 to 63, all different within a row; in each aligned block of 128 rows (0 to 127, 128 to 255, ...) at most 24 rows name the same one
- saved_hidden: bfloat16 [8, 64, 16, 24, 768], P('dp', 'expert'), may hold values from -6 to 6
- down_weight: bfloat16 [64, 2048, 768], P('expert'), may hold values from -0.21875 to 0.21875
- router_weight: bfloat16 [64, 2048], replicated, may hold values from -0.125 to 0.125
Outputs:
- hidden_grad: bfloat16 [8, 64, 16, 24, 768], P('dp', 'expert')
- down_grad: bfloat16 [64, 2048, 768], P('expert', 'dp')
- input_grad: bfloat16 [16384, 2048], P(('dp', 'expert'))
- router_grad: float32 [64, 2048], replicated
Inputs may be any that keep to these rules, and one draw needn't show every extreme that they name: `routes`: each token names 8 different experts; among the 128 tokens of one device no expert is named by more than 24 tokens, a bound that some block reaches. `combine`: each token's 8 weights are positive and sum to one.
All inputs are finite; a program needn't handle non-finite values.
Results may differ from a plain program's by a relative error of at most 0.017.
Values may be sent and summed in bfloat16 or wider, within the bound.
A program may use at most 128 MiB of HBM per device.

v0:
```python
import jax
import jax.numpy as jnp
from jax import lax
from jax.sharding import PartitionSpec as P


def make_marks(block_routes, total_experts):
    return block_routes[:, :, None] == jnp.arange(total_experts, dtype=jnp.int32)[None, None, :]


def slot_positions(route_marks):
    counts = jnp.sum(route_marks.astype(jnp.bfloat16), axis=1)
    token_order = jnp.arange(route_marks.shape[0], dtype=jnp.int32)
    earlier = (token_order[None, :] < token_order[:, None]).astype(jnp.bfloat16)
    before = jnp.dot(earlier, counts, preferred_element_type=jnp.float32)
    picked = jnp.sum(jnp.where(route_marks, before[:, None, :], 0.0), axis=2)
    return picked.astype(jnp.int32)


def pack_rows(scaled, lane_index, owner_slot, positions, local_experts, groups, capacity):
    width = scaled.shape[-1]
    flat_index = (owner_slot * groups + lane_index) * capacity + positions
    zero_rows = jnp.zeros((local_experts * groups * capacity, width), jnp.bfloat16)
    filled = zero_rows.at[flat_index.reshape(-1)].set(scaled.reshape(-1, width))
    return filled.reshape(local_experts, groups, capacity, width)


def local(inputs, out_grad, combine, routes, saved_hidden, down_weight, router_weight):
    token_count, width = out_grad.shape
    local_experts = down_weight.shape[0]
    total_experts = router_weight.shape[0]
    groups = lax.axis_size("expert")
    capacity = saved_hidden.shape[3]
    hidden_width = saved_hidden.shape[4]
    route_marks = make_marks(routes, total_experts)
    positions = slot_positions(route_marks)
    owner_dev = routes // local_experts
    owner_slot = routes % local_experts
    scaled = (combine[:, :, None] * out_grad[:, None, :].astype(jnp.float32)).astype(jnp.bfloat16)
    packed = pack_rows(scaled, owner_dev, owner_slot, positions, local_experts, groups, capacity)
    received = lax.all_to_all(packed, "expert", split_axis=1, concat_axis=1, tiled=True)
    hidden_local = saved_hidden[0]
    products_list = []
    hidden_list = []
    weight_terms = []
    for expert in range(local_experts):
        slot_rows = received[expert].reshape(groups * capacity, width)
        slot_acts = hidden_local[expert].reshape(groups * capacity, hidden_width)
        weight = down_weight[expert]
        recomputed = lax.dot_general(
            slot_acts, weight, (((1,), (1,)), ((), ())), preferred_element_type=jnp.float32
        )
        products_list.append(jnp.sum(recomputed * slot_rows.astype(jnp.float32), axis=1))
        hidden_list.append(
            jnp.dot(slot_rows, weight, preferred_element_type=jnp.float32).astype(jnp.bfloat16)
        )
        weight_terms.append(
            lax.dot_general(
                slot_rows, slot_acts, (((0,), (0,)), ((), ())), preferred_element_type=jnp.float32
            )
        )
    down_grad = lax.psum_scatter(
        jnp.stack(weight_terms).astype(jnp.bfloat16), "dp", scatter_dimension=1, tiled=True
    )
    hidden_grad = jnp.stack(hidden_list).reshape(1, local_experts, groups, capacity, hidden_width)
    slot_products = jnp.stack(products_list).reshape(local_experts, groups, capacity)
    returned = lax.all_to_all(slot_products, "expert", split_axis=1, concat_axis=1, tiled=True)
    pair_index = (owner_slot * groups + owner_dev) * capacity + positions
    pair_sums = returned.reshape(-1)[pair_index]
    logit_grad = pair_sums - combine * jnp.sum(pair_sums, axis=1, keepdims=True)
    dense_grad = jnp.sum(jnp.where(route_marks, logit_grad[:, :, None], 0.0), axis=1).astype(
        jnp.bfloat16
    )
    input_grad = jnp.dot(dense_grad, router_weight, preferred_element_type=jnp.float32).astype(
        jnp.bfloat16
    )
    router_part = lax.dot_general(
        dense_grad, inputs, (((0,), (0,)), ((), ())), preferred_element_type=jnp.float32
    )
    router_grad = lax.psum(router_part, ("dp", "expert"))
    return (hidden_grad, down_grad, input_grad, router_grad)


def solution(mesh):
    placed = (
        P(("dp", "expert"), None),
        P(("dp", "expert"), None),
        P(("dp", "expert"), None),
        P(("dp", "expert"), None),
        P("dp", "expert", None, None, None),
        P("expert", None, None),
        P(),
    )
    return jax.shard_map(
        local,
        mesh=mesh,
        in_specs=placed,
        out_specs=(
            P("dp", "expert", None, None, None),
            P("expert", "dp", None),
            P(("dp", "expert"), None),
            P(),
        ),
        check_vma=False,
    )
```

profile of v0, /device:TPU:1, one launch (start us, length us, event | category | flops | bytes accessed | tf_op | source)
XLA Modules:
  0.0 366.2 jit_solution(16921963926218966697)
XLA Ops:
  12.6 10.6 %scatter_custom_fusion = bf16[1536,2048]{1,0:T(8,128)(2,1)} fusion(s32[1024]{0:T(1024)S(1)} %bitcast.110, f32[128,2048]{1,0:T(8,128)S(1)} %convert_element_type.50, f32[1024]{0:T(1024)S(1)} %mul.48, bf16[]{:T(256)} %constant.31.clone.1), kind=kCustom, calls=%fused_computation.5 | custom fusion | flops 4194304 | bytes 7344130 | tf_op jit(solution)/shard_map/scatter | solution.py:24
  23.2 6.6 %copy.47 = bf16[4,16,24,2048]{3,2,0,1:T(8,128)(2,1)} copy(bf16[4,16,24,2048]{3,2,1,0:T(8,128)(2,1)} %bitcast.85) | data formatting | bytes 12582912 | tf_op jit(solution)/shard_map/reshape | solution.py:25
  29.8 7.8 %all-to-all-start = ((bf16[4,16,24,2048]{3,2,0,1:T(8,128)(2,1)}), bf16[4,16,24,2048]{3,2,0,1:T(8,128)(2,1)}, u32[]{:S(2)}, u32[]{:S(2)}) async-start(bf16[4,16,24,2048]{3,2,0,1:T(8,128)(2,1)} %copy.47), calls=%async_computation | async-start | bytes 12582912 | tf_op jit(solution)/shard_map/all_to_all | solution.py:41
  39.0 90.8 %all-to-all-done = bf16[4,16,24,2048]{3,2,0,1:T(8,128)(2,1)} async-done(((bf16[4,16,24,2048]{3,2,0,1:T(8,128)(2,1)}), bf16[4,16,24,2048]{3,2,0,1:T(8,128)(2,1)}, u32[]{:S(2)}, u32[]{:S(2)}) %all-to-all-start) | async-done | bytes 6291488 | tf_op jit(solution)/shard_map/all_to_all | solution.py:41
  129.9 4.8 %fusion.69 = (bf16[1,16,24,2048]{3,2,0,1:T(8,128)(2,1)S(1)}, bf16[1,16,24,2048]{3,2,0,1:T(8,128)(2,1)}, bf16[1,16,24,2048]{3,2,0,1:T(8,128)(2,1)S(1)}, bf16[1,16,24,2048]{3,2,0,1:T(8,128)(2,1)S(1)}) fusion(bf16[4,16,24,2048]{3,2,0,1:T(8,128)(2,1)} %all-to-all-done), kind=kLoop, calls=%fused_computation.80 | loop fusion | bytes 12582912 | tf_op jit(solution)/shard_map/slice | solution.py:47
  134.7 3.5 fusion.23
  138.2 3.6 multiply_reduce_fusion.2
  141.9 1.5 multiply_reduce_fusion.1
  143.4 3.5 fusion.24
  146.9 1.5 multiply_reduce_fusion.3
  148.4 3.5 fusion.22
  152.2 3.9 %multiply_reduce_fusion = f32[384]{0:T(512)S(1)} fusion(bf16[384,2048]{1,0:T(8,128)(2,1)} %bitcast.95, bf16[384,768]{1,0:T(8,128)(2,1)S(1)} %bitcast.98, bf16[4,2048,768]{2,1,0:T(8,128)(2,1)} %param.12), kind=kOutput, calls=%fused_computation.28 | convolution fusion | flops 1210318464 | bytes 5309952 | tf_op jit(solution)/shard_map/dot_general | solution.py:50
  156.9 5.4 %all-to-all-start.1 = ((f32[4,16,24]{2,0,1:T(4,128)}), f32[4,16,24]{2,0,1:T(4,128)S(1)}, u32[]{:S(2)}, u32[]{:S(2)}) async-start(f32[4,16,24]{2,0,1:T(4,128)} %pad_maximum_fusion.2), calls=%async_computation.2 | async-start | bytes 65536 | tf_op jit(solution)/shard_map/all_to_all | solution.py:67
  162.6 4.9 %fusion.25 = bf16[1,2048,768]{2,1,0:T(8,128)(2,1)} fusion(bf16[384,2048]{1,0:T(8,128)(2,1)} %bitcast.96, bf16[384,768]{1,0:T(8,128)(2,1)S(1)} %bitcast.99), kind=kOutput, calls=%fused_computation.36 | convolution fusion | flops 1209532416 | bytes 5308416 | tf_op jit(solution)/shard_map/dot_general | solution.py:58
  167.5 1.3 all-to-all-done.1
  168.8 6.2 %gather_fusion = f32[1024]{0:T(1024)S(1)} fusion(f32[1536]{0:T(1024)S(1)} %reshape.84, s32[1024]{0:T(1024)S(1)} %broadcast_clamp_fusion), kind=kCustom, calls=%fused_computation | custom fusion | bytes 12288 | tf_op jit(solution)/shard_map/gather | solution.py:69
  176.5 10.7 %pad_maximum_fusion = bf16[4,2048,768]{2,1,0:T(8,128)(2,1)} fusion(bf16[1,2048,768]{2,1,0:T(8,128)(2,1)} %fusion.25, bf16[1,2048,768]{2,1,0:T(8,128)(2,1)} %fusion.24, bf16[1,2048,768]{2,1,0:T(8,128)(2,1)} %fusion.23, bf16[1,2048,768]{2,1,0:T(8,128)(2,1)} %fusion.22), kind=kLoop, calls=%fused_computation.2 | loop fusion | flops 18874368 | bytes 25165824 | tf_op jit(solution)/shard_map/stack | solution.py:63
  187.2 3.9 %fusion.51 = bf16[384,768]{1,0:T(8,128)(2,1)S(1)} fusion(bf16[384,2048]{1,0:T(8,128)(2,1)} %bitcast.97, bf16[4,2048,768]{2,1,0:T(8,128)(2,1)} %param.12), kind=kOutput, calls=%fused_computation.50 | convolution fusion | flops 1208254464 | bytes 5308416 | tf_op jit(solution)/shard_map/dot_general | solution.py:55
  191.1 3.4 fusion.42
  194.6 3.3 fusion.48
  197.9 4.1 %fusion.45 = bf16[384,768]{1,0:T(8,128)(2,1)S(1)} fusion(bf16[384,2048]{1,0:T(8,128)(2,1)S(1)} %bitcast.88, bf16[4,2048,768]{2,1,0:T(8,128)(2,1)} %param.12), kind=kOutput, calls=%fused_computation.48 | convolution fusion | flops 1208254464 | bytes 5308416 | tf_op jit(solution)/shard_map/dot_general | solution.py:55
  202.0 1.7 pad_maximum_fusion.1
  204.9 152.0 %all-reduce.2.cloned.1.call-done = f32[64,2048]{1,0:T(8,128)} async-done(((f32[64,2048]{1,0:T(8,128)}), f32[64,2048]{1,0:T(8,128)}) %all-reduce.2.cloned.1.call-update) | async-done | bytes 524304 | tf_op jit(solution)/shard_map/psum | solution.py:80
  356.9 1.9 copy.52
  (64 shorter events, 10.0 us)
Async XLA Ops:
  8.0 167.4 %copy-start = (bf16[128,2048]{1,0:T(8,128)(2,1)S(1)}, bf16[128,2048]{1,0:T(8,128)(2,1)}, u32[]{:S(2)}) copy-start(bf16[128,2048]{1,0:T(8,128)(2,1)} %param.7) | copy-start | bytes 1572868
  29.8 8.0 %copy-start.1 = (bf16[1,4,16,24,768]{4,3,2,1,0:T(8,128)(2,1)S(1)}, bf16[1,4,16,24,768]{4,3,2,1,0:T(8,128)(2,1)}, u32[]{:S(2)}) copy-start(bf16[1,4,16,24,768]{4,3,2,1,0:T(8,128)(2,1)} %param.11) | copy-start | bytes 7077892
  29.8 100.1 %all-to-all-start = ((bf16[4,16,24,2048]{3,2,0,1:T(8,128)(2,1)}), bf16[4,16,24,2048]{3,2,0,1:T(8,128)(2,1)}, u32[]{:S(2)}, u32[]{:S(2)}) async-start(bf16[4,16,24,2048]{3,2,0,1:T(8,128)(2,1)} %copy.47), calls=%async_computation | async-start | bytes 12582912 | tf_op jit(solution)/shard_map/all_to_all | solution.py:41
  39.0 95.7 %copy-start.8 = (bf16[1,1,16,24,768]{4,3,2,1,0:T(8,128)(2,1)S(1)}, bf16[1,1,16,24,768]{4,3,2,1,0:T(8,128)(2,1)}, u32[]{:S(2)}) copy-start(bf16[1,1,16,24,768]{4,3,2,1,0:T(8,128)(2,1)} %get-tuple-element.11) | copy-start | bytes 1769476
  129.9 11.9 %slice-start = ((s8[12582912]{0:T(1024)(128)(4,1)}), s8[4194304]{0:T(1024)(128)(4,1)S(1)}, s32[]{:S(2)}) async-start(s8[12582912]{0:T(1024)(128)(4,1)} %bitcast.111), calls=%async_computation.5 | async-start | bytes 8388608
  129.9 11.9 %slice-start.1 = ((s8[12582912]{0:T(1024)(128)(4,1)}), s8[4194304]{0:T(1024)(128)(4,1)S(1)}, s32[]{:S(2)}) async-start(s8[12582912]{0:T(1024)(128)(4,1)} %bitcast.111), calls=%async_computation.6 | async-start | bytes 8388608
  134.7 8.7 %copy-start.2 = (bf16[1,16,24,2048]{3,2,0,1:T(8,128)(2,1)}, bf16[1,16,24,2048]{3,2,0,1:T(8,128)(2,1)S(1)}, u32[]{:S(2)}) copy-start(bf16[1,16,24,2048]{3,2,0,1:T(8,128)(2,1)S(1)} %get-tuple-element.8) | copy-start | bytes 4718596
  134.7 13.7 %copy-start.4 = (bf16[1,16,24,2048]{3,2,0,1:T(8,128)(2,1)}, bf16[1,16,24,2048]{3,2,0,1:T(8,128)(2,1)S(1)}, u32[]{:S(2)}) copy-start(bf16[1,16,24,2048]{3,2,0,1:T(8,128)(2,1)S(1)} %get-tuple-element.6) | copy-start | bytes 4718596
  138.2 3.6 copy-start.7
  138.2 3.6 slice-start.2
  143.4 3.5 copy-start.6
  156.9 11.8 %all-to-all-start.1 = ((f32[4,16,24]{2,0,1:T(4,128)}), f32[4,16,24]{2,0,1:T(4,128)S(1)}, u32[]{:S(2)}, u32[]{:S(2)}) async-start(f32[4,16,24]{2,0,1:T(4,128)} %pad_maximum_fusion.2), calls=%async_computation.2 | async-start | bytes 65536 | tf_op jit(solution)/shard_map/all_to_all | solution.py:67
  162.3 194.6 %all-reduce.2.cloned.1.call-start = ((), (), s32[]{:S(2)}) async-start(), calls=%async_computation.4 | async-start | bytes 1048576 | tf_op jit(solution)/shard_map/psum | solution.py:80
  168.8 6.5 %copy-start.11 = (f32[128,8]{0,1:T(8,128)S(1)}, f32[128,8]{0,1:T(8,128)}, u32[]{:S(2)}) copy-start(f32[128,8]{0,1:T(8,128)} %param.9) | copy-start | bytes 12292
  168.8 6.5 %copy-start.10 = (s32[128,8]{0,1:T(8,128)S(1)}, s32[128,8]{0,1:T(8,128)}, u32[]{:S(2)}) copy-start(s32[128,8]{0,1:T(8,128)} %param.10) | copy-start | bytes 12292
  176.4 180.5 %reduce-scatter.2.cloned.1.call-start = ((), (), s32[]{:S(2)}) async-start(), calls=%async_computation.3 | async-start | bytes 14155776 | tf_op jit(solution)/shard_map/reduce_scatter | solution.py:62
  187.2 3.9 %copy-start.5 = (bf16[1,16,24,2048]{3,2,0,1:T(8,128)(2,1)S(1)}, bf16[1,16,24,2048]{3,2,0,1:T(8,128)(2,1)}, u32[]{:S(2)}) copy-start(bf16[1,16,24,2048]{3,2,0,1:T(8,128)(2,1)} %copy-done.4) | copy-start | bytes 4718596
  191.1 3.5 copy-start.3
  202.0 1.7 copy-start.9
Sparse Core Ops, SparseCore 0:
  176.5 180.2 all-reduce.1
Sparse Core Ops, SparseCore 1:
  187.3 75.3 reduce-scatter.1
where the time goes:
time: 367 us; the launch traced here: 366 us
  waiting for transfers between devices  244 us (66%)
  matrix products  43 us (12%)
  other arithmetic  27.2 us (7%)
  local copies, waits for them, and re-layouts  22.6 us (6%)
  between operations  15.8 us (4%)
  starting transfers between devices  13.5 us (4%)
    psum x1, waiting for transfers between devices, local(): router_grad = lax.psum(router_part, ('dp', 'expert'))  152 us
    all_to_all x1, waiting for transfers between devices, local(): lax.all_to_all(packed, 'expert', split_axis=1, concat_axis=1, tiled=True)  90.8 us
    dot_general x4, matrix products, local(): lax.dot_general(slot_rows, slot_acts, (((0,), (0,)), ((), ())), preferred...  15.5 us
    dot_general x4, matrix products, local(): jnp.dot(slot_rows, weight, preferred_element_type=jnp.float32)  14.8 us
    another operation x1, other arithmetic, local(): jnp.stack(weight_terms).astype(jnp.bfloat16)  10.7 us
    scatter x1, other arithmetic, pack_rows(): filled = zero_rows.at[flat_index.reshape(-1)].set(scaled.reshape(-1, width))  10.6 us
    dot_general x4, matrix products, local(): lax.dot_general(slot_acts, weight, (((1,), (1,)), ((), ())), preferred_el...  10.5 us
    all_to_all x1, starting transfers between devices, local(): lax.all_to_all(packed, 'expert', split_axis=1, concat_axis=1, tiled=True)  7.77 us
  transfers between devices with their start and end apart: 4, of which 3 were waited for; matrix products, arithmetic and copies ran while one was open for 9% of the time, Pallas kernels for 0%

commit v1 on v0

v1 whole, which is shorter than its diff:
```python
import jax
import jax.numpy as jnp
from jax import lax
from jax.experimental import pallas as pl
from jax.experimental.pallas import tpu as pltpu
from jax.sharding import PartitionSpec as P

NX = 4
NY = 4
NZ = 4
NE = NX * NY
NDP = 2 * NZ
TICKS = 8
LANE = 128
BF = jnp.bfloat16
F32 = jnp.float32


def remote(src, dst, ssem, rsem, dev):
    return pltpu.make_async_remote_copy(
        src_ref=src, dst_ref=dst, send_sem=ssem, recv_sem=rsem,
        device_id=dev, device_id_type=pl.DeviceIdType.MESH,
    )


def fused(
    meta_hbm, og_hbm, hid_hbm, w_hbm, in_hbm, rw_hbm,
    hg_out, dw_out, ig_out, rp_out,
    G, W, H, HG, HGB, X, S, GAIN, META, CODES, GROW, DWS, RR, RSEND, RRECV,
    INP, RW, IG, RP,
    ag_s, ag_r, own_s, w_s, misc_s, dws_s, hgb_s, out_s, meta_s, meta_r, ret_s, ret_r,
):
    n_exp, slots, width_ff = hid_hbm.shape
    cap = slots // NE
    pair = 2 * cap
    me = lax.axis_index("expert")
    dp = lax.axis_index("dp")
    y, x = me // NX, lax.rem(me, NX)
    z, c = dp // 2, lax.rem(dp, 2)

    def expert_dev(index):
        return {"expert": index}

    def column(t, h):
        u = t // 2
        step = jnp.where(u == 0, 2, jnp.where(u == 1, 1, jnp.where(u == 2, 3, 0)))
        zz = lax.rem(z + step, NZ)
        core = 1 - c if h == 0 else c
        return pl.multiple_of((2 * zz + core) * 256 + lax.rem(t, 2) * LANE, LANE)

    def axes(h):
        return (x, y) if h == 0 else (y, x)

    def cell(t, h, a, b):
        return G.at[t, h, b, a] if h == 0 else G.at[t, h, a, b]

    def dev(h, a, b):
        return expert_dev(b * NX + a) if h == 0 else expert_dev(a * NX + b)

    def line(t, h, b, lo, n):
        return G.at[t, h, b, pl.ds(lo, n)] if h == 0 else G.at[t, h, pl.ds(lo, n), b]

    def up(i):
        return lax.rem(i + 1, 4)

    def down(i):
        return lax.rem(i + 3, 4)

    def far(i):
        return lax.rem(i + 2, 4)

    def hop(t, h, k):
        a, b = axes(h)
        if k == 0:
            return cell(t, h, a, b), cell(t, h, down(a), b), dev(h, up(a), b)
        if k == 1:
            return cell(t, h, a, b), cell(t, h, up(a), b), dev(h, down(a), b)
        if k == 2:
            lo = pl.ds(0, 64)
            return cell(t, h, down(a), b).at[lo], cell(t, h, far(a), b).at[lo], dev(h, up(a), b)
        if k == 3:
            hi = pl.ds(64, 64)
            return cell(t, h, up(a), b).at[hi], cell(t, h, far(a), b).at[hi], dev(h, down(a), b)
        if k == 4:
            return line(t, h, b, 0, 4), line(t, h, down(b), 0, 4), dev(h, a, up(b))
        if k == 5:
            return line(t, h, b, 0, 4), line(t, h, up(b), 0, 4), dev(h, a, down(b))
        if k == 6:
            return line(t, h, down(b), 0, 2), line(t, h, far(b), 0, 2), dev(h, a, up(b))
        return line(t, h, up(b), 2, 2), line(t, h, far(b), 2, 2), dev(h, a, down(b))

    def hop_start(t, h, k):
        sent, _, to = hop(t, h, k)
        remote(sent, sent, ag_s.at[t, h, k], ag_r.at[t, h, k], to).start()

    def hop_wait(t, h, k):
        _, got, to = hop(t, h, k)
        remote(got, got, ag_s.at[t, h, k], ag_r.at[t, h, k], to).wait_recv()

    def hop_drain(t, h, k):
        sent, _, to = hop(t, h, k)
        remote(sent, sent, ag_s.at[t, h, k], ag_r.at[t, h, k], to).wait_send()

    def own_copy(t, h):
        a, b = axes(h)
        return pltpu.make_async_copy(
            og_hbm.at[:, pl.ds(column(t, h), LANE)], cell(t, h, a, b), own_s.at[t, h]
        )

    def w_copy(t, h):
        return pltpu.make_async_copy(
            w_hbm.at[:, pl.ds(column(t, h), LANE), :], W.at[t, :, h], w_s.at[t, h]
        )

    def dw_copy(t, h):
        return pltpu.make_async_copy(
            DWS.at[lax.rem(t, 2), h], dw_out.at[:, pl.ds(column(t, h), LANE), :],
            dws_s.at[lax.rem(t, 2), h],
        )

    meta_own = pltpu.make_async_copy(meta_hbm, META.at[me], misc_s.at[0])
    meta_own.start()
    for t in range(TICKS):
        for h in range(2):
            own_copy(t, h).start()
    hid_copy = pltpu.make_async_copy(hid_hbm, H, misc_s.at[1])
    in_copy = pltpu.make_async_copy(in_hbm, INP, misc_s.at[2])
    rw_copy = pltpu.make_async_copy(rw_hbm, RW, misc_s.at[3])

    barrier = pltpu.get_barrier_semaphore()
    for d in range(1, NE):
        pl.semaphore_signal(barrier, inc=1, device_id=expert_dev(lax.rem(me + d, NE)),
                            device_id_type=pl.DeviceIdType.MESH)
    hid_copy.start()
    for t in range(TICKS):
        for h in range(2):
            w_copy(t, h).start()
    in_copy.start()
    rw_copy.start()
    pl.semaphore_wait(barrier, NE - 1)

    meta_own.wait()

    def plane_to(d):
        return expert_dev(lax.rem(me + d, NE))

    def plane_from(d):
        return lax.rem(me + NE - d, NE)

    def meta_send(d):
        return remote(META.at[me], META.at[me], meta_s.at[d], meta_r.at[d], plane_to(d))

    def meta_recv(d):
        got = META.at[plane_from(d)]
        return remote(got, got, meta_s.at[d], meta_r.at[d], plane_to(d))

    def build_dispatch():
        for d in range(1, NE):
            meta_recv(d).wait_recv()

        @pl.loop(0, NE // 2)
        def _(p):
            marks, gains = [], []
            for s2 in range(2):
                block = META[2 * p + s2]
                cb, rt = block[0:8], block[8:16]
                for e in range(n_exp):
                    hit = rt == (me * n_exp + e).astype(F32)
                    marks.append(jnp.sum(jnp.where(hit, 1.0, 0.0), axis=0, keepdims=True))
                    gains.append(jnp.sum(jnp.where(hit, cb, 0.0), axis=0, keepdims=True))
            at = pl.multiple_of(p * 8, 8)
            CODES[pl.ds(at, 8), :] = jnp.concatenate(marks, axis=0)
            GROW[pl.ds(at, 8), :] = jnp.concatenate(gains, axis=0)

        marks = CODES[...]
        r = lax.broadcasted_iota(jnp.int32, (LANE, LANE), 0)
        q = lax.broadcasted_iota(jnp.int32, (LANE, LANE), 1)
        earlier = jnp.where(r < q, 1.0, 0.0).astype(BF)
        before = jnp.dot(marks.astype(BF), earlier, preferred_element_type=F32)
        CODES[...] = jnp.where(marks > 0.5, before, -1000.0)

        @pl.loop(0, NE // 2)
        def _(p):
            at = pl.multiple_of(p * 8, 8)
            codes = CODES[pl.ds(at, 8), :]
            gains = GROW[pl.ds(at, 8), :]
            place = lax.broadcasted_iota(jnp.int32, (pair, LANE), 0).astype(F32)
            for e in range(n_exp):
                first = jnp.where(place == codes[e:e + 1], 1.0, 0.0)
                second = jnp.where(place - cap == codes[n_exp + e:n_exp + e + 1], 1.0, 0.0)
                S[p, e * pair:(e + 1) * pair, 0:LANE] = first.astype(BF)
                S[p, e * pair:(e + 1) * pair, LANE:2 * LANE] = second.astype(BF)
                gain = jnp.sum(
                    first * gains[e:e + 1] + second * gains[n_exp + e:n_exp + e + 1],
                    axis=1, keepdims=True,
                )
                GAIN[p, e * pair:(e + 1) * pair, :] = jnp.broadcast_to(gain, (pair, LANE))

    def compute(t):
        for h in range(2):
            w_copy(t, h).wait()
        for p in range(NE // 2):
            yy, xx = p // 2, 2 * (p % 2)
            g0 = G[t, 0, yy, xx:xx + 2].reshape(2 * LANE, LANE)
            g1 = G[t, 1, yy, xx:xx + 2].reshape(2 * LANE, LANE)
            rows = jnp.dot(S[p], jnp.concatenate([g0, g1], axis=1), preferred_element_type=F32)
            gain = GAIN[p]
            rows = (rows * jnp.concatenate([gain, gain], axis=1)).astype(BF)
            for e in range(n_exp):
                X[e, p * pair:(p + 1) * pair, :] = rows[e * pair:(e + 1) * pair]

        @pl.when(t >= 2)
        def _():
            for h in range(2):
                dw_copy(t - 2, h).wait()

        @pl.loop(0, n_exp)
        def _(e):
            xe = X[e]
            we = W[t, e].reshape(2 * LANE, width_ff)
            HG[e] += jnp.dot(xe, we, preferred_element_type=F32)
            grad = lax.dot_general(xe, H[e], (((0,), (0,)), ((), ())), preferred_element_type=F32)
            DWS[lax.rem(t, 2), 0, e] = grad[:LANE].astype(BF)
            DWS[lax.rem(t, 2), 1, e] = grad[LANE:].astype(BF)

        for h in range(2):
            dw_copy(t, h).start()

    @pl.loop(0, TICKS + 4)
    def _(i):
        @pl.when(i < TICKS)
        def _():
            for h in range(2):
                own_copy(i, h).wait()
                hop_start(i, h, 0)
                hop_start(i, h, 1)

        @pl.when(i == 0)
        def _():
            for d in range(1, NE):
                meta_send(d).start()
            hid_copy.wait()
            HG[...] = jnp.zeros_like(HG)

        for phase in range(3):
            @pl.when((i > phase) & (i <= TICKS + phase))
            def _(phase=phase):
                t = i - 1 - phase
                for h in range(2):
                    for k in (2 * phase, 2 * phase + 1):
                        hop_wait(t, h, k)
                        if phase != 1:
                            hop_start(t, h, k + 2)
                if phase == 1:
                    for h in range(2):
                        hop_start(t, h, 4)
                        hop_start(t, h, 5)

        @pl.when(i == 3)
        def _():
            build_dispatch()

        @pl.when(i >= 4)
        def _():
            t = i - 4
            for h in range(2):
                hop_wait(t, h, 6)
                hop_wait(t, h, 7)
            compute(t)

    for e in range(n_exp):
        hg = HG[e]
        HGB[e] = hg.astype(BF)
        pltpu.make_async_copy(HGB.at[e], hg_out.at[e], hgb_s.at[e]).start()
        prod = jnp.sum(H[e].astype(F32) * hg, axis=1, keepdims=True)
        for p in range(NE // 2):
            row = jnp.sum(
                S[p, e * pair:(e + 1) * pair, :].astype(F32) * prod[p * pair:(p + 1) * pair],
                axis=0, keepdims=True,
            )
            RR[p, e:e + 1, :] = row
            RR[p, n_exp + e:n_exp + e + 1, :] = row
    half = lax.broadcasted_iota(jnp.int32, (8, LANE), 0) // n_exp
    mine = half == lax.rem(me, 2)
    for p in range(NE // 2):
        for s2 in range(2):
            RSEND[2 * p + s2] = jnp.where(mine, RR[p, :, s2 * LANE:(s2 + 1) * LANE], 0.0)

    def ret_send(d):
        out = RSEND.at[lax.rem(me + d, NE)]
        return remote(out, RRECV.at[me], ret_s.at[d], ret_r.at[d], plane_to(d))

    def ret_recv(d):
        got = RRECV.at[plane_from(d)]
        return remote(got, got, ret_s.at[d], ret_r.at[d], plane_to(d))

    for d in range(1, NE):
        ret_send(d).start()
    RRECV[me] = RSEND[me]

    own_meta = META[me]
    expert_id = lax.broadcasted_iota(jnp.int32, (NE * n_exp, LANE), 0).astype(F32)
    gate = jnp.zeros((NE * n_exp, LANE), F32)
    named = jnp.zeros((NE * n_exp, LANE), F32)
    for k in range(8):
        hit = expert_id == own_meta[8 + k:9 + k]
        gate += jnp.where(hit, own_meta[k:k + 1], 0.0)
        named += jnp.where(hit, 1.0, 0.0)

    in_copy.wait()
    rw_copy.wait()
    for d in range(1, NE):
        ret_recv(d).wait_recv()
    sums = jnp.concatenate([RRECV[2 * q] + RRECV[2 * q + 1] for q in range(NE // 2)], axis=0)
    total = jnp.sum(sums, axis=0, keepdims=True)
    dense = jnp.where(named > 0.5, sums - gate * total, 0.0).astype(BF)
    for q in range(4):
        cols = slice(q * 512, (q + 1) * 512)
        IG[:, cols] = lax.dot_general(
            dense, RW[:, cols], (((0,), (0,)), ((), ())), preferred_element_type=F32
        ).astype(BF)
        RP[:, cols] = jnp.dot(dense, INP[:, cols], preferred_element_type=F32)
    ig_copy = pltpu.make_async_copy(IG, ig_out, out_s.at[0])
    rp_copy = pltpu.make_async_copy(RP, rp_out, out_s.at[1])
    ig_copy.start()
    rp_copy.start()

    @pl.loop(0, TICKS)
    def _(t):
        for h in range(2):
            for k in range(8):
                hop_drain(t, h, k)

    for d in range(1, NE):
        meta_send(d).wait_send()
        ret_send(d).wait_send()
    for t in (TICKS - 2, TICKS - 1):
        for h in range(2):
            dw_copy(t, h).wait()
    for e in range(n_exp):
        pltpu.make_async_copy(HGB.at[e], hg_out.at[e], hgb_s.at[e]).wait()
    ig_copy.wait()
    rp_copy.wait()


def local(inputs, out_grad, combine, routes, saved_hidden, down_weight, router_weight):
    tokens, width = out_grad.shape
    n_exp, _, ff = down_weight.shape
    total = router_weight.shape[0]
    slots = saved_hidden.shape[2] * saved_hidden.shape[3]
    pair = slots // (NE // 2)
    meta = jnp.concatenate([combine.T, routes.T.astype(F32)], axis=0)
    hidden = saved_hidden.reshape(n_exp, slots, ff)
    dma = pltpu.SemaphoreType.DMA
    hg, dw, ig, rp = pl.pallas_call(
        fused,
        out_shape=(
            jax.ShapeDtypeStruct((n_exp, slots, ff), BF),
            jax.ShapeDtypeStruct((n_exp, width, ff), BF),
            jax.ShapeDtypeStruct((tokens, width), BF),
            jax.ShapeDtypeStruct((total, width), F32),
        ),
        in_specs=[pl.BlockSpec(memory_space=pl.ANY)] * 6,
        out_specs=(pl.BlockSpec(memory_space=pl.ANY),) * 4,
        scratch_shapes=[
            pltpu.VMEM((TICKS, 2, NY, NX, tokens, LANE), BF),
            pltpu.VMEM((TICKS, n_exp, 2, LANE, ff), BF),
            pltpu.VMEM((n_exp, slots, ff), BF),
            pltpu.VMEM((n_exp, slots, ff), F32),
            pltpu.VMEM((n_exp, slots, ff), BF),
            pltpu.VMEM((n_exp, slots, 2 * LANE), BF),
            pltpu.VMEM((NE // 2, n_exp * pair, 2 * LANE), BF),
            pltpu.VMEM((NE // 2, n_exp * pair, LANE), F32),
            pltpu.VMEM((NE, 16, LANE), F32),
            pltpu.VMEM((NE * n_exp, LANE), F32),
            pltpu.VMEM((NE * n_exp, LANE), F32),
            pltpu.VMEM((2, 2, n_exp, LANE, ff), BF),
            pltpu.VMEM((NE // 2, 8, 2 * LANE), F32),
            pltpu.VMEM((NE, 8, LANE), F32),
            pltpu.VMEM((NE, 8, LANE), F32),
            pltpu.VMEM((tokens, width), BF),
            pltpu.VMEM((total, width), BF),
            pltpu.VMEM((tokens, width), BF),
            pltpu.VMEM((total, width), F32),
            dma((TICKS, 2, 8)),
            dma((TICKS, 2, 8)),
            dma((TICKS, 2)),
            dma((TICKS, 2)),
            dma((4,)),
            dma((2, 2)),
            dma((n_exp,)),
            dma((2,)),
            dma((NE,)),
            dma((NE,)),
            dma((NE,)),
            dma((NE,)),
        ],
        compiler_params=pltpu.CompilerParams(
            collective_id=0, has_side_effects=True, vmem_limit_bytes=60 * 2**20
        ),
        name="moe_down_backward",
    )(meta, out_grad, hidden, down_weight, inputs, router_weight)
    down_grad = lax.psum_scatter(dw, "dp", scatter_dimension=1, tiled=True)
    router_grad = lax.psum(rp, ("dp", "expert"))
    return hg.reshape(saved_hidden.shape), down_grad, ig, router_grad


def solution(mesh):
    placed = (
        P(("dp", "expert"), None),
        P(("dp", "expert"), None),
        P(("dp", "expert"), None),
        P(("dp", "expert"), None),
        P("dp", "expert", None, None, None),
        P("expert", None, None),
        P(),
    )
    return jax.shard_map(
        local,
        mesh=mesh,
        in_specs=placed,
        out_specs=(
            P("dp", "expert", None, None, None),
            P("expert", "dp", None),
            P(("dp", "expert"), None),
            P(),
        ),
        check_vma=False,
    )
```

time: 367 us -> 269 us (0.73)
  Pallas kernels: 0 us -> 65.3 us
  waiting for transfers between devices: 244 us -> 183 us
  matrix products: 43 us -> 0 us
  other arithmetic: 27.2 us -> 1.98 us
  local copies, waits for them, and re-layouts: 22.6 us -> 3 us
  starting transfers between devices: 13.5 us -> 0.08 us
    all_to_all x2 -> x0, waiting for transfers between devices: 92.1 us -> none  [the longest x1 90.8 us: local(): lax.all_to_all(packed, 'expert', split_axis=1, concat_axis=1, tiled=True)]
    pallas_call x0 -> x1, Pallas kernels: none -> 65.3 us  [local(): pl.pallas_call(fused, out_shape=(jax.ShapeDtypeStruct((n_exp, slots, ff),...]
    dot_general x15 -> x0, matrix products: 43 us -> none  [the longest x4 15.5 us: local(): lax.dot_general(slot_rows, slot_acts, (((0,), (0,)), ((), ())), preferred...]
    psum x1, waiting for transfers between devices: 152 us -> 183 us  [local(): router_grad = lax.psum(rp, ('dp', 'expert'))]
    all_to_all x2 -> x0, starting transfers between devices: 13.2 us -> none  [the longest x1 7.77 us: local(): lax.all_to_all(packed, 'expert', split_axis=1, concat_axis=1, tiled=True)]
    another operation x3 -> x0, other arithmetic: 13.1 us -> none  [the longest x1 10.7 us: local(): jnp.stack(weight_terms).astype(jnp.bfloat16)]
    scatter x1 -> x0, other arithmetic: 10.6 us -> none  [pack_rows(): filled = zero_rows.at[flat_index.reshape(-1)].set(scaled.reshape(-1, width))]
    reshape x3 -> x0, local copies, waits for them, and re-layouts: 6.75 us -> none  [the longest x1 6.57 us: pack_rows(): return filled.reshape(local_experts, groups, capacity, width)]
  transfers between devices with their start and end apart: 4 -> 2, of which waited for: 3 -> 1; matrix products, arithmetic and copies ran while one was open for 9% -> 0% of each run, Pallas kernels for 0% -> 0%
where the time goes in v1:
time: 269 us
  waiting for transfers between devices  183 us (68%)
  Pallas kernels  65.3 us (24%)
  between operations  15.5 us (6%)
  local copies, waits for them, and re-layouts  3 us (1%)
    psum x1, waiting for transfers between devices, local(): router_grad = lax.psum(rp, ('dp', 'expert'))  183 us
    pallas_call x1, Pallas kernels, local(): pl.pallas_call(fused, out_shape=(jax.ShapeDtypeStruct((n_exp, slots, ff),...  65.3 us
  transfers between devices with their start and end apart: 2, of which 1 were waited for; matrix products, arithmetic and copies ran while one was open for 0% of the time, Pallas kernels for 0%

profile of v1, /device:TPU:1, one launch (start us, length us, event | category | flops | bytes accessed | tf_op | source)
XLA Modules:
  0.0 268.9 jit_solution(12174192103617543781)
XLA Ops:
  8.0 0.0 all-reduce.2.cloned.1.call-start
  8.0 0.7 convert_bitcast_fusion
  8.7 1.3 pad_maximum_fusion.meta_hbm
  10.0 65.3 %moe_down_backward.1 = (bf16[4,384,768]{2,1,0:T(8,128)(2,1)}, bf16[4,2048,768]{2,1,0:T(8,128)(2,1)}, bf16[128,2048]{1,0:T(8,128)(2,1)}, f32[64,2048]{1,0:T(8,128)}) custom-call(f32[16,128]{1,0:T(8,128)} %pad_maximum_fusion.meta_hbm, bf16[128,2048]{1,0:T(8,128)(2,1)} %og_hbm.1, bf16[4,384,768]{2,1,0:T(8,128)(2,1)} %bitcast.5, bf16[4,2048,768]{2,1,0:T(8,128)(2,1)} %w_hbm.1, ...), custom_call_target="tpu_custom_call" | custom-call | tf_op jit(solution)/shard_map/moe_down_backward/pallas_call | solution.py:355
  75.3 0.0 all-reduce.2.cloned.1.call-update
  75.3 0.0 reduce-scatter.2.cloned.1.call-start
  75.4 0.0 copy-start
  75.4 0.5 reduce-scatter.2.cloned.1.call-update
  75.9 0.0 copy-start.1
  75.9 182.5 %all-reduce.2.cloned.1.call-done = f32[64,2048]{1,0:T(8,128)} async-done(((f32[64,2048]{1,0:T(8,128)}), f32[64,2048]{1,0:T(8,128)}) %all-reduce.2.cloned.1.call-update) | async-done | bytes 524304 | tf_op jit(solution)/shard_map/psum | solution.py:404
  258.4 0.0 copy-start.2
  258.4 0.0 reduce-scatter.2.cloned.1.call-done
  258.4 0.0 copy-done
  258.4 1.4 copy.15
  259.8 0.0 copy-done.1
  259.8 0.8 copy.16
  260.6 0.0 copy-done.2
  260.6 0.8 copy.17
Async XLA Ops:
  8.0 250.4 %all-reduce.2.cloned.1.call-start = ((), (), s32[]{:S(2)}) async-start(), calls=%async_computation.2 | async-start | bytes 1048576 | tf_op jit(solution)/shard_map/psum | solution.py:404
  75.3 183.1 %reduce-scatter.2.cloned.1.call-start = ((), (), s32[]{:S(2)}) async-start(), calls=%async_computation.1 | async-start | bytes 14155776 | tf_op jit(solution)/shard_map/reduce_scatter | solution.py:403
  75.4 183.1 %copy-start = (bf16[4,384,768]{2,1,0:T(8,128)(2,1)S(1)}, bf16[4,384,768]{2,1,0:T(8,128)(2,1)}, u32[]{:S(2)}) copy-start(bf16[4,384,768]{2,1,0:T(8,128)(2,1)} %get-tuple-element.8) | copy-start | bytes 7077892
  75.9 183.9 %copy-start.1 = (bf16[128,2048]{1,0:T(8,128)(2,1)S(1)}, bf16[128,2048]{1,0:T(8,128)(2,1)}, u32[]{:S(2)}) copy-start(bf16[128,2048]{1,0:T(8,128)(2,1)} %get-tuple-element.18) | copy-start | bytes 1572868
  258.4 2.2 copy-start.2
Sparse Core Ops, SparseCore 0:
  75.4 182.9 all-reduce.1
Sparse Core Ops, SparseCore 1:
  78.8 77.0 reduce-scatter.1

commit v2 on v1

--- a/solution.py
+++ b/solution.py
@@ -26,9 +26,10 @@
 def fused(
     meta_hbm, og_hbm, hid_hbm, w_hbm, in_hbm, rw_hbm,
     hg_out, dw_out, ig_out, rp_out,
-    G, W, H, HG, HGB, X, S, GAIN, META, CODES, GROW, DWS, RR, RSEND, RRECV,
-    INP, RW, IG, RP,
-    ag_s, ag_r, own_s, w_s, misc_s, dws_s, hgb_s, out_s, meta_s, meta_r, ret_s, ret_r,
+    G, W, H, HG, X, S, GAIN, META, CODES, GROW, RR, RSEND, RRECV,
+    CS, CR, OWN, ZA, ZB, ZC, ZD, INP, RW, IG, RP, R1, R2, OUT,
+    ag_s, ag_r, own_s, w_s, misc_s, hg_s, out_s, meta_s, meta_r, ret_s, ret_r,
+    core_s, core_r, z_s, z_r, r1_s, r1_r, r2_s, r2_r, r3_s, r3_r,
 ):
     n_exp, slots, width_ff = hid_hbm.shape
     cap = slots // NE
@@ -112,11 +113,80 @@
             w_hbm.at[:, pl.ds(column(t, h), LANE), :], W.at[t, :, h], w_s.at[t, h]
         )
 
-    def dw_copy(t, h):
+    def dp_dev(index):
+        return {"dp": index}
+
+    next_z = dp_dev(2 * lax.rem(z + 1, NZ) + c)
+    prev_z = dp_dev(2 * lax.rem(z + 3, NZ) + c)
+
+    def core_hop(t):
+        return remote(
+            CS.at[lax.rem(t, 2)], CR.at[t], core_s.at[t], core_r.at[t], dp_dev(2 * z + 1 - c)
+        )
+
+    def z_hop(v, k):
+        t = v if k < 2 else (2 + v if k == 2 else 4 + v)
+        if k == 0:
+            sent, land = OWN.at[t, pl.ds(0, 2)], ZA.at[v]
+        elif k == 1:
+            sent, land = OWN.at[t, pl.ds(2, 2)], ZB.at[v]
+        else:
+            sent, land = OWN.at[t], (ZC.at[v] if k == 2 else ZD.at[v])
+        return remote(sent, land, z_s.at[v, k], z_r.at[v, k], next_z if k in (0, 2) else prev_z)
+
+    def add_blocks(t, lo, others):
+        for e in range(lo, lo + 2):
+            acc = OWN[t, e].astype(F32)
+            for other in others(e):
+                acc += other.astype(F32)
+            OWN[t, e] = acc.astype(BF)
+
+    def pair_up(t):
+        core_hop(t).wait_recv()
+        v, u = lax.rem(t, 2), t // 2
+
+        @pl.when(u != 1)
+        def _():
+            add_blocks(t, 0, lambda e: [CR[t, e]])
+
+        @pl.when(u == 1)
+        def _():
+            z_hop(v, 0).wait_recv()
+            add_blocks(t, 0, lambda e: [CR[t, e], ZA[v, e]])
+
+        @pl.when(u != 2)
+        def _():
+            add_blocks(t, 2, lambda e: [CR[t, e]])
+
+        @pl.when(u == 2)
+        def _():
+            z_hop(v, 1).wait_recv()
+            add_blocks(t, 2, lambda e: [CR[t, e], ZB[v, e - 2]])
+
+        @pl.when(u == 0)
+        def _():
+            z_hop(v, 0).start()
+            z_hop(v, 1).start()
+
+        @pl.when(u == 1)
+        def _():
+            z_hop(v, 2).start()
+
+        @pl.when(u == 2)
+        def _():
+            z_hop(v, 3).start()
+
+    def dw_copy(v):
         return pltpu.make_async_copy(
-            DWS.at[lax.rem(t, 2), h], dw_out.at[:, pl.ds(column(t, h), LANE), :],
-            dws_s.at[lax.rem(t, 2), h],
+            OWN.at[6 + v], dw_out.at[:, pl.ds(v * LANE, LANE), :], out_s.at[2 + v]
         )
+
+    def finish_down(v):
+        z_hop(v, 2).wait_recv()
+        z_hop(v, 3).wait_recv()
+        for lo in (0, 2):
+            add_blocks(6 + v, lo, lambda e: [ZC[v, e], ZD[v, e]])
+        dw_copy(v).start()
 
     meta_own = pltpu.make_async_copy(meta_hbm, META.at[me], misc_s.at[0])
     meta_own.start()
@@ -131,13 +201,16 @@
     for d in range(1, NE):
         pl.semaphore_signal(barrier, inc=1, device_id=expert_dev(lax.rem(me + d, NE)),
                             device_id_type=pl.DeviceIdType.MESH)
+    for d in range(1, NDP):
+        pl.semaphore_signal(barrier, inc=1, device_id=dp_dev(lax.rem(dp + d, NDP)),
+                            device_id_type=pl.DeviceIdType.MESH)
     hid_copy.start()
     for t in range(TICKS):
         for h in range(2):
             w_copy(t, h).start()
     in_copy.start()
     rw_copy.start()
-    pl.semaphore_wait(barrier, NE - 1)
+    pl.semaphore_wait(barrier, NE - 1 + NDP - 1)
 
     meta_own.wait()
 
@@ -211,8 +284,7 @@
 
         @pl.when(t >= 2)
         def _():
-            for h in range(2):
-                dw_copy(t - 2, h).wait()
+            core_hop(t - 2).wait_send()
 
         @pl.loop(0, n_exp)
         def _(e):
@@ -220,11 +292,10 @@
             we = W[t, e].reshape(2 * LANE, width_ff)
             HG[e] += jnp.dot(xe, we, preferred_element_type=F32)
             grad = lax.dot_general(xe, H[e], (((0,), (0,)), ((), ())), preferred_element_type=F32)
-            DWS[lax.rem(t, 2), 0, e] = grad[:LANE].astype(BF)
-            DWS[lax.rem(t, 2), 1, e] = grad[LANE:].astype(BF)
-
-        for h in range(2):
-            dw_copy(t, h).start()
+            CS[lax.rem(t, 2), e] = grad[:LANE].astype(BF)
+            OWN[t, e] = grad[LANE:].astype(BF)
+
+        core_hop(t).start()
 
     @pl.loop(0, TICKS + 4)
     def _(i):
@@ -260,6 +331,10 @@
         def _():
             build_dispatch()
 
+        @pl.when(i >= 5)
+        def _():
+            pair_up(i - 5)
+
         @pl.when(i >= 4)
         def _():
             t = i - 4
@@ -270,8 +345,8 @@
 
     for e in range(n_exp):
         hg = HG[e]
-        HGB[e] = hg.astype(BF)
-        pltpu.make_async_copy(HGB.at[e], hg_out.at[e], hgb_s.at[e]).start()
+        for q in range(3):
+            W[e, q // 2, q % 2] = hg[q * LANE:(q + 1) * LANE].astype(BF)
         prod = jnp.sum(H[e].astype(F32) * hg, axis=1, keepdims=True)
         for p in range(NE // 2):
             row = jnp.sum(
@@ -298,6 +373,16 @@
         ret_send(d).start()
     RRECV[me] = RSEND[me]
 
+    def hg_copy(e, q):
+        return pltpu.make_async_copy(
+            W.at[e, q // 2, q % 2], hg_out.at[e, pl.ds(q * LANE, LANE)], hg_s.at[e, q]
+        )
+
+    for e in range(n_exp):
+        for q in range(3):
+            hg_copy(e, q).start()
+    pair_up(TICKS - 1)
+
     own_meta = META[me]
     expert_id = lax.broadcasted_iota(jnp.int32, (NE * n_exp, LANE), 0).astype(F32)
     gate = jnp.zeros((NE * n_exp, LANE), F32)
@@ -316,14 +401,71 @@
     dense = jnp.where(named > 0.5, sums - gate * total, 0.0).astype(BF)
     for q in range(4):
         cols = slice(q * 512, (q + 1) * 512)
+        part = jnp.dot(dense, INP[:, cols], preferred_element_type=F32)
+        for j in range(4):
+            RP[4 * q + j] = part[:, j * LANE:(j + 1) * LANE]
+
+    def r1_send(d):
+        return remote(RP.at[lax.rem(me + d, NE)], R1.at[me], r1_s.at[d], r1_r.at[d], plane_to(d))
+
+    def r1_recv(d):
+        got = R1.at[plane_from(d)]
+        return remote(got, got, r1_s.at[d], r1_r.at[d], plane_to(d))
+
+    def r2_send(d):
+        to = dp_dev(lax.rem(dp + d, NDP))
+        return remote(R2.at[dp], R2.at[dp], r2_s.at[d], r2_r.at[d], to)
+
+    def r2_recv(d):
+        got = R2.at[lax.rem(dp + NDP - d, NDP)]
+        return remote(got, got, r2_s.at[d], r2_r.at[d], dp_dev(lax.rem(dp + d, NDP)))
+
+    def r3_send(d):
+        return remote(OUT.at[me], OUT.at[me], r3_s.at[d], r3_r.at[d], plane_to(d))
+
+    def r3_recv(d):
+        got = OUT.at[plane_from(d)]
+        return remote(got, got, r3_s.at[d], r3_r.at[d], plane_to(d))
+
+    for d in range(1, NE):
+        r1_send(d).start()
+    R1[me] = RP[me]
+    for q in range(4):
+        cols = slice(q * 512, (q + 1) * 512)
         IG[:, cols] = lax.dot_general(
             dense, RW[:, cols], (((0,), (0,)), ((), ())), preferred_element_type=F32
         ).astype(BF)
-        RP[:, cols] = jnp.dot(dense, INP[:, cols], preferred_element_type=F32)
     ig_copy = pltpu.make_async_copy(IG, ig_out, out_s.at[0])
-    rp_copy = pltpu.make_async_copy(RP, rp_out, out_s.at[1])
     ig_copy.start()
-    rp_copy.start()
+
+    for d in range(1, NE):
+        r1_recv(d).wait_recv()
+    acc = R1[0]
+    for j in range(1, NE):
+        acc += R1[j]
+    R2[dp] = acc
+    for d in range(1, NDP):
+        r2_send(d).start()
+    finish_down(0)
+    for d in range(1, NDP):
+        r2_recv(d).wait_recv()
+    acc = R2[0]
+    for j in range(1, NDP):
+        acc += R2[j]
+    OUT[me] = acc
+    for d in range(1, NE):
+        r3_send(d).start()
+    finish_down(1)
+    for d in range(1, NE):
+        r3_recv(d).wait_recv()
+
+    def rp_copy(j):
+        return pltpu.make_async_copy(
+            OUT.at[j], rp_out.at[:, pl.ds(j * LANE, LANE)], misc_s.at[4 + j]
+        )
+
+    for j in range(NE):
+        rp_copy(j).start()
 
     @pl.loop(0, TICKS)
     def _(t):
@@ -334,13 +476,22 @@
     for d in range(1, NE):
         meta_send(d).wait_send()
         ret_send(d).wait_send()
-    for t in (TICKS - 2, TICKS - 1):
-        for h in range(2):
-            dw_copy(t, h).wait()
+        r1_send(d).wait_send()
+        r3_send(d).wait_send()
+    for d in range(1, NDP):
+        r2_send(d).wait_send()
+    core_hop(TICKS - 2).wait_send()
+    core_hop(TICKS - 1).wait_send()
+    for v in range(2):
+        for k in range(4):
+            z_hop(v, k).wait_send()
+        dw_copy(v).wait()
     for e in range(n_exp):
-        pltpu.make_async_copy(HGB.at[e], hg_out.at[e], hgb_s.at[e]).wait()
+        for q in range(3):
+            hg_copy(e, q).wait()
     ig_copy.wait()
-    rp_copy.wait()
+    for j in range(NE):
+        rp_copy(j).wait()
 
 
 def local(inputs, out_grad, combine, routes, saved_hidden, down_weight, router_weight):
@@ -356,7 +507,7 @@
         fused,
         out_shape=(
             jax.ShapeDtypeStruct((n_exp, slots, ff), BF),
-            jax.ShapeDtypeStruct((n_exp, width, ff), BF),
+            jax.ShapeDtypeStruct((n_exp, width // NDP, ff), BF),
             jax.ShapeDtypeStruct((tokens, width), BF),
             jax.ShapeDtypeStruct((total, width), F32),
         ),
@@ -367,31 +518,48 @@
             pltpu.VMEM((TICKS, n_exp, 2, LANE, ff), BF),
             pltpu.VMEM((n_exp, slots, ff), BF),
             pltpu.VMEM((n_exp, slots, ff), F32),
-            pltpu.VMEM((n_exp, slots, ff), BF),
             pltpu.VMEM((n_exp, slots, 2 * LANE), BF),
             pltpu.VMEM((NE // 2, n_exp * pair, 2 * LANE), BF),
             pltpu.VMEM((NE // 2, n_exp * pair, LANE), F32),
             pltpu.VMEM((NE, 16, LANE), F32),
             pltpu.VMEM((NE * n_exp, LANE), F32),
             pltpu.VMEM((NE * n_exp, LANE), F32),
-            pltpu.VMEM((2, 2, n_exp, LANE, ff), BF),
             pltpu.VMEM((NE // 2, 8, 2 * LANE), F32),
             pltpu.VMEM((NE, 8, LANE), F32),
             pltpu.VMEM((NE, 8, LANE), F32),
+            pltpu.VMEM((2, n_exp, LANE, ff), BF),
+            pltpu.VMEM((TICKS, n_exp, LANE, ff), BF),
+            pltpu.VMEM((TICKS, n_exp, LANE, ff), BF),
+            pltpu.VMEM((2, 2, LANE, ff), BF),
+            pltpu.VMEM((2, 2, LANE, ff), BF),
+            pltpu.VMEM((2, n_exp, LANE, ff), BF),
+            pltpu.VMEM((2, n_exp, LANE, ff), BF),
             pltpu.VMEM((tokens, width), BF),
             pltpu.VMEM((total, width), BF),
             pltpu.VMEM((tokens, width), BF),
-            pltpu.VMEM((total, width), F32),
+            pltpu.VMEM((NE, total, LANE), F32),
+            pltpu.VMEM((NE, total, LANE), F32),
+            pltpu.VMEM((NDP, total, LANE), F32),
+            pltpu.VMEM((NE, total, LANE), F32),
             dma((TICKS, 2, 8)),
             dma((TICKS, 2, 8)),
             dma((TICKS, 2)),
             dma((TICKS, 2)),
+            dma((4 + NE,)),
+            dma((n_exp, 3)),
             dma((4,)),
-            dma((2, 2)),
-            dma((n_exp,)),
-            dma((2,)),
-            dma((NE,)),
-            dma((NE,)),
+            dma((NE,)),
+            dma((NE,)),
+            dma((NE,)),
+            dma((NE,)),
+            dma((TICKS,)),
+            dma((TICKS,)),
+            dma((2, 4)),
+            dma((2, 4)),
+            dma((NE,)),
+            dma((NE,)),
+            dma((NDP,)),
+            dma((NDP,)),
             dma((NE,)),
             dma((NE,)),
         ],
@@ -400,9 +568,7 @@
         ),
         name="moe_down_backward",
     )(meta, out_grad, hidden, down_weight, inputs, router_weight)
-    down_grad = lax.psum_scatter(dw, "dp", scatter_dimension=1, tiled=True)
-    router_grad = lax.psum(rp, ("dp", "expert"))
-    return hg.reshape(saved_hidden.shape), down_grad, ig, router_grad
+    return hg.reshape(saved_hidden.shape), dw, ig, rp
 
 
 def solution(mesh):

time: 269 us -> 115 us (0.43)
  waiting for transfers between devices: 183 us -> 0 us
  Pallas kernels: 65.3 us -> 106 us
  between operations: 15.5 us -> 0.65 us
  local copies, waits for them, and re-layouts: 3 us -> 6.3 us
    psum x1 -> x0, waiting for transfers between devices: 183 us -> none  [local(): router_grad = lax.psum(rp, ('dp', 'expert'))]
    pallas_call x1, Pallas kernels: 65.3 us -> 106 us  [local(): pl.pallas_call(fused, out_shape=(jax.ShapeDtypeStruct((n_exp, slots, ff),...]
    unnamed x9 -> x10, local copies, waits for them, and re-layouts: 3 us -> 6.3 us
  transfers between devices with their start and end apart: 2 -> 0, of which waited for: 1 -> 0; matrix products, arithmetic and copies ran while one was open for 0% -> 0% of each run, Pallas kernels for 0% -> 0%
where the time goes in v2:
time: 115 us
  Pallas kernels  106 us (92%)
  local copies, waits for them, and re-layouts  6.3 us (5%)
  other arithmetic  1.98 us (2%)
    pallas_call x1, Pallas kernels, local(): pl.pallas_call(fused, out_shape=(jax.ShapeDtypeStruct((n_exp, slots, ff),...  106 us
    unnamed x10, local copies, waits for them, and re-layouts  6.3 us

profile of v2, /device:TPU:1, one launch (start us, length us, event | category | flops | bytes accessed | tf_op | source)
XLA Modules:
  0.0 115.0 jit_solution(4037923862231173291)
XLA Ops:
  0.6 0.7 convert_bitcast_fusion
  1.3 1.3 %pad_maximum_fusion.meta_hbm = f32[16,128]{1,0:T(8,128)} fusion(f32[8,128]{1,0:T(8,128)S(1)} %convert_bitcast_fusion, f32[8,128]{1,0:T(8,128)} %bitcast.7), kind=kLoop, calls=%fused_computation | loop fusion | flops 2048 | bytes 16384 | tf_op jit(solution)/shard_map/concatenate | solution.py:503
  2.6 106.1 %moe_down_backward.1 = (bf16[4,384,768]{2,1,0:T(8,128)(2,1)}, bf16[4,256,768]{2,1,0:T(8,128)(2,1)}, bf16[128,2048]{1,0:T(8,128)(2,1)}, f32[64,2048]{1,0:T(8,128)}) custom-call(f32[16,128]{1,0:T(8,128)} %pad_maximum_fusion.meta_hbm, bf16[128,2048]{1,0:T(8,128)(2,1)} %og_hbm.1, bf16[4,384,768]{2,1,0:T(8,128)(2,1)} %bitcast.5, bf16[4,2048,768]{2,1,0:T(8,128)(2,1)} %w_hbm.1, ...), custom_call_target="tpu_custom_call" | custom-call | tf_op jit(solution)/shard_map/moe_down_backward/pallas_call | solution.py:506
  108.7 0.0 copy-start
  108.7 3.3 %copy.15 = bf16[1,4,16,24,768]{4,3,2,1,0:T(8,128)(2,1)} copy(bf16[1,4,16,24,768]{4,3,2,1,0:T(8,128)(2,1)} %bitcast.6) | data formatting | bytes 4718592
  112.0 0.0 copy-done
  112.0 0.0 copy-start.2
  112.1 0.0 copy-start.1
  112.1 1.1 copy.16
  113.2 0.2 copy-done.2
  113.4 0.8 copy.17
  114.2 0.0 copy-done.1
  114.2 0.8 copy.18
Async XLA Ops:
  108.7 3.4 %copy-start = (bf16[4,256,768]{2,1,0:T(8,128)(2,1)S(1)}, bf16[4,256,768]{2,1,0:T(8,128)(2,1)}, u32[]{:S(2)}) copy-start(bf16[4,256,768]{2,1,0:T(8,128)(2,1)} %get-tuple-element.17) | copy-start | bytes 4718596
  112.0 1.4 %copy-start.2 = (bf16[128,2048]{1,0:T(8,128)(2,1)S(1)}, bf16[128,2048]{1,0:T(8,128)(2,1)}, u32[]{:S(2)}) copy-start(bf16[128,2048]{1,0:T(8,128)(2,1)} %get-tuple-element.18) | copy-start | bytes 1572868
  112.1 2.2 %copy-start.1 = (f32[64,2048]{1,0:T(8,128)S(1)}, f32[64,2048]{1,0:T(8,128)}, u32[]{:S(2)}) copy-start(f32[64,2048]{1,0:T(8,128)} %get-tuple-element.19) | copy-start | bytes 1572868

commit v3 on v2

--- a/solution.py
+++ b/solution.py
@@ -24,12 +24,12 @@
 
 
 def fused(
-    meta_hbm, og_hbm, hid_hbm, w_hbm, in_hbm, rw_hbm,
+    comb_hbm, route_hbm, og_hbm, hid_hbm, w_hbm, in_hbm, rw_hbm,
     hg_out, dw_out, ig_out, rp_out,
-    G, W, H, HG, X, S, GAIN, META, CODES, GROW, RR, RSEND, RRECV,
-    CS, CR, OWN, ZA, ZB, ZC, ZD, INP, RW, IG, RP, R1, R2, OUT,
+    G, W, H, HG, X, S, GAIN, META, ROUTE, CODES, GROW, RR, RSEND, RRECV,
+    CS, CR, OWN, ZA, ZB, ZC, ZD, INP, RW, IG, RP, RC, R1, R2, OUT,
     ag_s, ag_r, own_s, w_s, misc_s, hg_s, out_s, meta_s, meta_r, ret_s, ret_r,
-    core_s, core_r, z_s, z_r, r1_s, r1_r, r2_s, r2_r, r3_s, r3_r,
+    core_s, core_r, z_s, z_r, r1_s, r1_r, r2_s, r2_r, r3_s, r3_r, rc_s, rc_r, rp_s,
 ):
     n_exp, slots, width_ff = hid_hbm.shape
     cap = slots // NE
@@ -43,11 +43,11 @@
         return {"expert": index}
 
     def column(t, h):
-        u = t // 2
-        step = jnp.where(u == 0, 2, jnp.where(u == 1, 1, jnp.where(u == 2, 3, 0)))
+        step = jnp.where(t < 2, 2, jnp.where(t >= 6, 0, 1 + 2 * lax.rem(t, 2)))
+        v = jnp.where(t < 2, t, jnp.where(t >= 6, t - 6, (t - 2) // 2))
         zz = lax.rem(z + step, NZ)
         core = 1 - c if h == 0 else c
-        return pl.multiple_of((2 * zz + core) * 256 + lax.rem(t, 2) * LANE, LANE)
+        return pl.multiple_of((2 * zz + core) * 256 + v * LANE, LANE)
 
     def axes(h):
         return (x, y) if h == 0 else (y, x)
@@ -119,13 +119,14 @@
     next_z = dp_dev(2 * lax.rem(z + 1, NZ) + c)
     prev_z = dp_dev(2 * lax.rem(z + 3, NZ) + c)
 
-    def core_hop(t):
+    def core_hop(t, e):
         return remote(
-            CS.at[lax.rem(t, 2)], CR.at[t], core_s.at[t], core_r.at[t], dp_dev(2 * z + 1 - c)
+            CS.at[lax.rem(t, 2), e], CR.at[t, e], core_s.at[t, e], core_r.at[t, e],
+            dp_dev(2 * z + 1 - c),
         )
 
     def z_hop(v, k):
-        t = v if k < 2 else (2 + v if k == 2 else 4 + v)
+        t = v if k < 2 else k + 2 * v
         if k == 0:
             sent, land = OWN.at[t, pl.ds(0, 2)], ZA.at[v]
         elif k == 1:
@@ -141,39 +142,36 @@
                 acc += other.astype(F32)
             OWN[t, e] = acc.astype(BF)
 
+    def core_wait(t, lo):
+        for e in (lo, lo + 1):
+            core_hop(t, e).wait_recv()
+
     def pair_up(t):
-        core_hop(t).wait_recv()
-        v, u = lax.rem(t, 2), t // 2
-
-        @pl.when(u != 1)
-        def _():
+        @pl.when(t < 2)
+        def _():
+            for k in range(2):
+                core_wait(t, 2 * k)
+                add_blocks(t, 2 * k, lambda e: [CR[t, e]])
+                z_hop(t, k).start()
+
+        @pl.when((t == 2) | (t == 4))
+        def _():
+            v = (t - 2) // 2
+            z_hop(v, 0).wait_recv()
+            core_wait(t, 0)
+            add_blocks(t, 0, lambda e: [CR[t, e], ZA[v, e]])
+            core_wait(t, 2)
+            add_blocks(t, 2, lambda e: [CR[t, e]])
+            z_hop(v, 2).start()
+
+        @pl.when((t == 3) | (t == 5))
+        def _():
+            v = (t - 2) // 2
+            core_wait(t, 0)
             add_blocks(t, 0, lambda e: [CR[t, e]])
-
-        @pl.when(u == 1)
-        def _():
-            z_hop(v, 0).wait_recv()
-            add_blocks(t, 0, lambda e: [CR[t, e], ZA[v, e]])
-
-        @pl.when(u != 2)
-        def _():
-            add_blocks(t, 2, lambda e: [CR[t, e]])
-
-        @pl.when(u == 2)
-        def _():
             z_hop(v, 1).wait_recv()
+            core_wait(t, 2)
             add_blocks(t, 2, lambda e: [CR[t, e], ZB[v, e - 2]])
-
-        @pl.when(u == 0)
-        def _():
-            z_hop(v, 0).start()
-            z_hop(v, 1).start()
-
-        @pl.when(u == 1)
-        def _():
-            z_hop(v, 2).start()
-
-        @pl.when(u == 2)
-        def _():
             z_hop(v, 3).start()
 
     def dw_copy(v):
@@ -185,11 +183,14 @@
         z_hop(v, 2).wait_recv()
         z_hop(v, 3).wait_recv()
         for lo in (0, 2):
-            add_blocks(6 + v, lo, lambda e: [ZC[v, e], ZD[v, e]])
+            core_wait(6 + v, lo)
+            add_blocks(6 + v, lo, lambda e: [CR[6 + v, e], ZC[v, e], ZD[v, e]])
         dw_copy(v).start()
 
-    meta_own = pltpu.make_async_copy(meta_hbm, META.at[me], misc_s.at[0])
-    meta_own.start()
+    comb_own = pltpu.make_async_copy(comb_hbm, META.at[me, pl.ds(0, 8)], misc_s.at[0])
+    route_own = pltpu.make_async_copy(route_hbm, ROUTE, misc_s.at[4])
+    comb_own.start()
+    route_own.start()
     for t in range(TICKS):
         for h in range(2):
             own_copy(t, h).start()
@@ -210,9 +211,10 @@
             w_copy(t, h).start()
     in_copy.start()
     rw_copy.start()
+    comb_own.wait()
+    route_own.wait()
+    META[me, 8:16, :] = ROUTE[...].astype(F32)
     pl.semaphore_wait(barrier, NE - 1 + NDP - 1)
-
-    meta_own.wait()
 
     def plane_to(d):
         return expert_dev(lax.rem(me + d, NE))
@@ -227,12 +229,11 @@
         got = META.at[plane_from(d)]
         return remote(got, got, meta_s.at[d], meta_r.at[d], plane_to(d))
 
-    def build_dispatch():
+    def build_codes():
         for d in range(1, NE):
             meta_recv(d).wait_recv()
 
-        @pl.loop(0, NE // 2)
-        def _(p):
+        for p in range(NE // 2):
             marks, gains = [], []
             for s2 in range(2):
                 block = META[2 * p + s2]
@@ -241,9 +242,8 @@
                     hit = rt == (me * n_exp + e).astype(F32)
                     marks.append(jnp.sum(jnp.where(hit, 1.0, 0.0), axis=0, keepdims=True))
                     gains.append(jnp.sum(jnp.where(hit, cb, 0.0), axis=0, keepdims=True))
-            at = pl.multiple_of(p * 8, 8)
-            CODES[pl.ds(at, 8), :] = jnp.concatenate(marks, axis=0)
-            GROW[pl.ds(at, 8), :] = jnp.concatenate(gains, axis=0)
+            CODES[8 * p:8 * p + 8, :] = jnp.concatenate(marks, axis=0)
+            GROW[8 * p:8 * p + 8, :] = jnp.concatenate(gains, axis=0)
 
         marks = CODES[...]
         r = lax.broadcasted_iota(jnp.int32, (LANE, LANE), 0)
@@ -252,12 +252,11 @@
         before = jnp.dot(marks.astype(BF), earlier, preferred_element_type=F32)
         CODES[...] = jnp.where(marks > 0.5, before, -1000.0)
 
-        @pl.loop(0, NE // 2)
-        def _(p):
-            at = pl.multiple_of(p * 8, 8)
-            codes = CODES[pl.ds(at, 8), :]
-            gains = GROW[pl.ds(at, 8), :]
-            place = lax.broadcasted_iota(jnp.int32, (pair, LANE), 0).astype(F32)
+    def build_dispatch():
+        place = lax.broadcasted_iota(jnp.int32, (pair, LANE), 0).astype(F32)
+        for p in range(NE // 2):
+            codes = CODES[8 * p:8 * p + 8, :]
+            gains = GROW[8 * p:8 * p + 8, :]
             for e in range(n_exp):
                 first = jnp.where(place == codes[e:e + 1], 1.0, 0.0)
                 second = jnp.where(place - cap == codes[n_exp + e:n_exp + e + 1], 1.0, 0.0)
@@ -282,66 +281,97 @@
             for e in range(n_exp):
                 X[e, p * pair:(p + 1) * pair, :] = rows[e * pair:(e + 1) * pair]
 
-        @pl.when(t >= 2)
-        def _():
-            core_hop(t - 2).wait_send()
-
         @pl.loop(0, n_exp)
         def _(e):
             xe = X[e]
             we = W[t, e].reshape(2 * LANE, width_ff)
             HG[e] += jnp.dot(xe, we, preferred_element_type=F32)
             grad = lax.dot_general(xe, H[e], (((0,), (0,)), ((), ())), preferred_element_type=F32)
+
+            @pl.when(t >= 2)
+            def _():
+                core_hop(t - 2, e).wait_send()
+
             CS[lax.rem(t, 2), e] = grad[:LANE].astype(BF)
+            core_hop(t, e).start()
             OWN[t, e] = grad[LANE:].astype(BF)
 
-        core_hop(t).start()
-
-    @pl.loop(0, TICKS + 4)
-    def _(i):
-        @pl.when(i < TICKS)
-        def _():
-            for h in range(2):
-                own_copy(i, h).wait()
-                hop_start(i, h, 0)
-                hop_start(i, h, 1)
-
-        @pl.when(i == 0)
-        def _():
-            for d in range(1, NE):
-                meta_send(d).start()
-            hid_copy.wait()
-            HG[...] = jnp.zeros_like(HG)
-
-        for phase in range(3):
-            @pl.when((i > phase) & (i <= TICKS + phase))
-            def _(phase=phase):
-                t = i - 1 - phase
-                for h in range(2):
-                    for k in (2 * phase, 2 * phase + 1):
-                        hop_wait(t, h, k)
-                        if phase != 1:
-                            hop_start(t, h, k + 2)
-                if phase == 1:
-                    for h in range(2):
-                        hop_start(t, h, 4)
-                        hop_start(t, h, 5)
-
-        @pl.when(i == 3)
-        def _():
-            build_dispatch()
-
-        @pl.when(i >= 5)
-        def _():
-            pair_up(i - 5)
-
-        @pl.when(i >= 4)
-        def _():
-            t = i - 4
-            for h in range(2):
-                hop_wait(t, h, 6)
-                hop_wait(t, h, 7)
-            compute(t)
+            @pl.when(e == 0)
+            def _():
+                gather_ahead(t)
+
+    def phase_start(t, phase):
+        for h in range(2):
+            if phase == 0:
+                own_copy(t, h).wait()
+            hop_start(t, h, 2 * phase)
+            hop_start(t, h, 2 * phase + 1)
+
+    def phase_wait(t, phase):
+        for h in range(2):
+            hop_wait(t, h, 2 * phase)
+            hop_wait(t, h, 2 * phase + 1)
+
+    def gather_ahead(t):
+        @pl.when(t + 1 < TICKS)
+        def _():
+            phase_wait(t + 1, 2)
+            phase_start(t + 1, 3)
+
+        @pl.when(t + 3 < TICKS)
+        def _():
+            phase_wait(t + 3, 1)
+            phase_start(t + 3, 2)
+
+        @pl.when(t + 5 < TICKS)
+        def _():
+            phase_wait(t + 5, 0)
+            phase_start(t + 5, 1)
+
+        @pl.when(t + 7 < TICKS)
+        def _():
+            phase_start(t + 7, 0)
+
+    phase_start(0, 0)
+    phase_start(1, 0)
+    for d in range(1, NE):
+        meta_send(d).start()
+    phase_wait(0, 0)
+    phase_start(0, 1)
+    phase_start(2, 0)
+    phase_wait(0, 1)
+    phase_start(0, 2)
+    phase_wait(1, 0)
+    phase_start(1, 1)
+    phase_start(3, 0)
+    HG[...] = jnp.zeros_like(HG)
+    build_codes()
+    phase_wait(2, 0)
+    phase_start(2, 1)
+    phase_start(4, 0)
+    phase_wait(0, 2)
+    phase_start(0, 3)
+    phase_wait(1, 1)
+    phase_start(1, 2)
+    phase_start(5, 0)
+    phase_wait(3, 0)
+    phase_start(3, 1)
+    build_dispatch()
+    phase_wait(2, 1)
+    phase_start(2, 2)
+    phase_wait(4, 0)
+    phase_start(4, 1)
+    phase_start(6, 0)
+    hid_copy.wait()
+
+    @pl.loop(0, TICKS)
+    def _(t):
+        phase_wait(t, 3)
+        compute(t)
+
+        @pl.when(t < 6)
+        def _():
+            pair_up(t)
 
     for e in range(n_exp):
         hg = HG[e]
@@ -381,7 +411,6 @@
     for e in range(n_exp):
         for q in range(3):
             hg_copy(e, q).start()
-    pair_up(TICKS - 1)
 
     own_meta = META[me]
     expert_id = lax.broadcasted_iota(jnp.int32, (NE * n_exp, LANE), 0).astype(F32)
@@ -399,37 +428,56 @@
     sums = jnp.concatenate([RRECV[2 * q] + RRECV[2 * q + 1] for q in range(NE // 2)], axis=0)
     total = jnp.sum(sums, axis=0, keepdims=True)
     dense = jnp.where(named > 0.5, sums - gate * total, 0.0).astype(BF)
+    rows_half = NE * n_exp // 2
     for q in range(4):
         cols = slice(q * 512, (q + 1) * 512)
         part = jnp.dot(dense, INP[:, cols], preferred_element_type=F32)
         for j in range(4):
-            RP[4 * q + j] = part[:, j * LANE:(j + 1) * LANE]
+            block = part[:, j * LANE:(j + 1) * LANE]
+            RP[4 * q + j, 0] = block[:rows_half]
+            RP[4 * q + j, 1] = block[rows_half:]
+
+    other = dp_dev(2 * z + 1 - c)
+
+    def rc_send():
+        return remote(RP.at[:, 1 - c], RC, rc_s.at[0], rc_r.at[0], other)
 
     def r1_send(d):
-        return remote(RP.at[lax.rem(me + d, NE)], R1.at[me], r1_s.at[d], r1_r.at[d], plane_to(d))
+        out = RP.at[lax.rem(me + d, NE), c]
+        return remote(out, R1.at[me], r1_s.at[d], r1_r.at[d], plane_to(d))
 
     def r1_recv(d):
         got = R1.at[plane_from(d)]
         return remote(got, got, r1_s.at[d], r1_r.at[d], plane_to(d))
 
     def r2_send(d):
-        to = dp_dev(lax.rem(dp + d, NDP))
-        return remote(R2.at[dp], R2.at[dp], r2_s.at[d], r2_r.at[d], to)
+        to = dp_dev(2 * lax.rem(z + d, NZ) + c)
+        return remote(R2.at[z], R2.at[z], r2_s.at[d], r2_r.at[d], to)
 
     def r2_recv(d):
-        got = R2.at[lax.rem(dp + NDP - d, NDP)]
-        return remote(got, got, r2_s.at[d], r2_r.at[d], dp_dev(lax.rem(dp + d, NDP)))
+        got = R2.at[lax.rem(z + NZ - d, NZ)]
+        return remote(got, got, r2_s.at[d], r2_r.at[d], dp_dev(2 * lax.rem(z + d, NZ) + c))
 
     def r3_send(d):
-        return remote(OUT.at[me], OUT.at[me], r3_s.at[d], r3_r.at[d], plane_to(d))
+        return remote(OUT.at[me, c], OUT.at[me, c], r3_s.at[d], r3_r.at[d], plane_to(d))
 
     def r3_recv(d):
-        got = OUT.at[plane_from(d)]
+        got = OUT.at[plane_from(d), c]
         return remote(got, got, r3_s.at[d], r3_r.at[d], plane_to(d))
 
+    def r4_send():
+        return remote(OUT.at[:, c], OUT.at[:, c], rc_s.at[1], rc_r.at[1], other)
+
+    def r4_recv():
+        return remote(OUT.at[:, 1 - c], OUT.at[:, 1 - c], rc_s.at[1], rc_r.at[1], other)
+
+    rc_send().start()
+    rc_send().wait_recv()
+    for j in range(NE):
+        RP[j, c] += RC[j]
     for d in range(1, NE):
         r1_send(d).start()
-    R1[me] = RP[me]
+    R1[me] = RP[me, c]
     for q in range(4):
         cols = slice(q * 512, (q + 1) * 512)
         IG[:, cols] = lax.dot_general(
@@ -443,29 +491,34 @@
     acc = R1[0]
     for j in range(1, NE):
         acc += R1[j]
-    R2[dp] = acc
-    for d in range(1, NDP):
+    R2[z] = acc
+    for d in range(1, NZ):
         r2_send(d).start()
     finish_down(0)
-    for d in range(1, NDP):
+    for d in range(1, NZ):
         r2_recv(d).wait_recv()
     acc = R2[0]
-    for j in range(1, NDP):
+    for j in range(1, NZ):
         acc += R2[j]
-    OUT[me] = acc
+    OUT[me, c] = acc
     for d in range(1, NE):
         r3_send(d).start()
     finish_down(1)
     for d in range(1, NE):
         r3_recv(d).wait_recv()
-
-    def rp_copy(j):
+    r4_send().start()
+    r4_recv().wait_recv()
+
+    def rp_copy(j, half):
         return pltpu.make_async_copy(
-            OUT.at[j], rp_out.at[:, pl.ds(j * LANE, LANE)], misc_s.at[4 + j]
+            OUT.at[j, half],
+            rp_out.at[pl.ds(half * rows_half, rows_half), pl.ds(j * LANE, LANE)],
+            rp_s.at[j, half],
         )
 
     for j in range(NE):
-        rp_copy(j).start()
+        rp_copy(j, 0).start()
+        rp_copy(j, 1).start()
 
     @pl.loop(0, TICKS)
     def _(t):
@@ -478,10 +531,13 @@
         ret_send(d).wait_send()
         r1_send(d).wait_send()
         r3_send(d).wait_send()
-    for d in range(1, NDP):
+    for d in range(1, NZ):
         r2_send(d).wait_send()
-    core_hop(TICKS - 2).wait_send()
-    core_hop(TICKS - 1).wait_send()
+    rc_send().wait_send()
+    r4_send().wait_send()
+    for e in range(n_exp):
+        core_hop(TICKS - 2, e).wait_send()
+        core_hop(TICKS - 1, e).wait_send()
     for v in range(2):
         for k in range(4):
             z_hop(v, k).wait_send()
@@ -491,7 +547,8 @@
             hg_copy(e, q).wait()
     ig_copy.wait()
     for j in range(NE):
-        rp_copy(j).wait()
+        rp_copy(j, 0).wait()
+        rp_copy(j, 1).wait()
 
 
 def local(inputs, out_grad, combine, routes, saved_hidden, down_weight, router_weight):
@@ -500,19 +557,18 @@
     total = router_weight.shape[0]
     slots = saved_hidden.shape[2] * saved_hidden.shape[3]
     pair = slots // (NE // 2)
-    meta = jnp.concatenate([combine.T, routes.T.astype(F32)], axis=0)
     hidden = saved_hidden.reshape(n_exp, slots, ff)
     dma = pltpu.SemaphoreType.DMA
     hg, dw, ig, rp = pl.pallas_call(
         fused,
         out_shape=(
-            jax.ShapeDtypeStruct((n_exp, slots, ff), BF),
-            jax.ShapeDtypeStruct((n_exp, width // NDP, ff), BF),
-            jax.ShapeDtypeStruct((tokens, width), BF),
-            jax.ShapeDtypeStruct((total, width), F32),
+            pltpu.VMEM((n_exp, slots, ff), BF),
+            pltpu.VMEM((n_exp, width // NDP, ff), BF),
+            pltpu.VMEM((tokens, width), BF),
+            pltpu.VMEM((total, width), F32),
         ),
-        in_specs=[pl.BlockSpec(memory_space=pl.ANY)] * 6,
-        out_specs=(pl.BlockSpec(memory_space=pl.ANY),) * 4,
+        in_specs=[pl.BlockSpec(memory_space=pl.ANY)] * 7,
+        out_specs=(pl.BlockSpec(memory_space=pltpu.VMEM),) * 4,
         scratch_shapes=[
             pltpu.VMEM((TICKS, 2, NY, NX, tokens, LANE), BF),
             pltpu.VMEM((TICKS, n_exp, 2, LANE, ff), BF),
@@ -522,6 +578,7 @@
             pltpu.VMEM((NE // 2, n_exp * pair, 2 * LANE), BF),
             pltpu.VMEM((NE // 2, n_exp * pair, LANE), F32),
             pltpu.VMEM((NE, 16, LANE), F32),
+            pltpu.VMEM((8, LANE), jnp.int32),
             pltpu.VMEM((NE * n_exp, LANE), F32),
             pltpu.VMEM((NE * n_exp, LANE), F32),
             pltpu.VMEM((NE // 2, 8, 2 * LANE), F32),
@@ -537,37 +594,41 @@
             pltpu.VMEM((tokens, width), BF),
             pltpu.VMEM((total, width), BF),
             pltpu.VMEM((tokens, width), BF),
-            pltpu.VMEM((NE, total, LANE), F32),
-            pltpu.VMEM((NE, total, LANE), F32),
-            pltpu.VMEM((NDP, total, LANE), F32),
-            pltpu.VMEM((NE, total, LANE), F32),
+            pltpu.VMEM((NE, 2, total // 2, LANE), F32),
+            pltpu.VMEM((NE, total // 2, LANE), F32),
+            pltpu.VMEM((NE, total // 2, LANE), F32),
+            pltpu.VMEM((NZ, total // 2, LANE), F32),
+            pltpu.VMEM((NE, 2, total // 2, LANE), F32),
             dma((TICKS, 2, 8)),
             dma((TICKS, 2, 8)),
             dma((TICKS, 2)),
             dma((TICKS, 2)),
-            dma((4 + NE,)),
+            dma((5,)),
             dma((n_exp, 3)),
             dma((4,)),
             dma((NE,)),
             dma((NE,)),
             dma((NE,)),
             dma((NE,)),
-            dma((TICKS,)),
-            dma((TICKS,)),
+            dma((TICKS, n_exp)),
+            dma((TICKS, n_exp)),
             dma((2, 4)),
             dma((2, 4)),
             dma((NE,)),
             dma((NE,)),
-            dma((NDP,)),
-            dma((NDP,)),
-            dma((NE,)),
-            dma((NE,)),
+            dma((NZ,)),
+            dma((NZ,)),
+            dma((NE,)),
+            dma((NE,)),
+            dma((2,)),
+            dma((2,)),
+            dma((NE, 2)),
         ],
         compiler_params=pltpu.CompilerParams(
-            collective_id=0, has_side_effects=True, vmem_limit_bytes=60 * 2**20
+            collective_id=0, has_side_effects=True, vmem_limit_bytes=58 * 2**20
         ),
         name="moe_down_backward",
-    )(meta, out_grad, hidden, down_weight, inputs, router_weight)
+    )(combine.T, routes.T, out_grad, hidden, down_weight, inputs, router_weight)
     return hg.reshape(saved_hidden.shape), dw, ig, rp
 
 

time: 115 us -> 103 us (0.90)
  Pallas kernels: 106 us -> 98.2 us
  local copies, waits for them, and re-layouts: 6.3 us -> 4.14 us
  other arithmetic: 1.98 us -> 0 us
    pallas_call x1, Pallas kernels: 106 us -> 98.2 us  [local(): pl.pallas_call(fused, out_shape=(pltpu.VMEM((n_exp, slots, ff), BF), pltp...]
    unnamed x10 -> x4, local copies, waits for them, and re-layouts: 6.3 us -> 4.14 us
    concatenate x1 -> x0, other arithmetic: 1.29 us -> none  [local(): meta = jnp.concatenate([combine.T, routes.T.astype(F32)], axis=0)]
where the time goes in v3:
time: 103 us
  Pallas kernels  98.2 us (95%)
  local copies, waits for them, and re-layouts  4.14 us (4%)
    pallas_call x1, Pallas kernels, local(): pl.pallas_call(fused, out_shape=(pltpu.VMEM((n_exp, slots, ff), BF), pltp...  98.2 us
    unnamed x4, local copies, waits for them, and re-layouts  4.14 us

profile of v3, /device:TPU:1, one launch (start us, length us, event | category | flops | bytes accessed | tf_op | source)
XLA Modules:
  0.0 103.0 jit_solution(12418538834517728514)
XLA Ops:
  0.6 98.2 %moe_down_backward.1 = (bf16[4,384,768]{2,1,0:T(8,128)(2,1)S(1)}, bf16[4,256,768]{2,1,0:T(8,128)(2,1)S(1)}, bf16[128,2048]{1,0:T(8,128)(2,1)S(1)}, f32[64,2048]{1,0:T(8,128)S(1)}) custom-call(f32[8,128]{1,0:T(8,128)} %bitcast.6, s32[8,128]{1,0:T(8,128)} %bitcast.7, bf16[128,2048]{1,0:T(8,128)(2,1)} %og_hbm.1, bf16[4,384,768]{2,1,0:T(8,128)(2,1)} %bitcast.5, ...), custom_call_target="tpu_custom_call" | custom-call | tf_op jit(solution)/shard_map/moe_down_backward/pallas_call | solution.py:562
  98.9 1.4 %copy.15 = bf16[1,4,16,24,768]{4,3,2,1,0:T(8,128)(2,1)} copy(bf16[1,4,16,24,768]{4,3,2,1,0:T(8,128)(2,1)S(1)} %bitcast.4) | data formatting | bytes 4718592
  100.3 0.8 copy.17
  101.1 0.8 copy.18
  101.9 1.1 %copy.16 = bf16[4,256,768]{2,1,0:T(8,128)(2,1)} copy(bf16[4,256,768]{2,1,0:T(8,128)(2,1)S(1)} %get-tuple-element.13) | data formatting | bytes 3145728

commit v4 on v3

--- a/solution.py
+++ b/solution.py
@@ -26,10 +26,10 @@
 def fused(
     comb_hbm, route_hbm, og_hbm, hid_hbm, w_hbm, in_hbm, rw_hbm,
     hg_out, dw_out, ig_out, rp_out,
-    G, W, H, HG, X, S, GAIN, META, ROUTE, CODES, GROW, RR, RSEND, RRECV,
-    CS, CR, OWN, ZA, ZB, ZC, ZD, INP, RW, IG, RP, RC, R1, R2, OUT,
-    ag_s, ag_r, own_s, w_s, misc_s, hg_s, out_s, meta_s, meta_r, ret_s, ret_r,
-    core_s, core_r, z_s, z_r, r1_s, r1_r, r2_s, r2_r, r3_s, r3_r, rc_s, rc_r, rp_s,
+    G, W, H, HG, X, S, GAIN, META, ROUTE, CODES, GROW, CS, CR, OWN, ZA, ZB, ZC, ZD,
+    INP, INC, RW, GATE, PROD, PSB, SUMS, DENSE, PF, R2, OUT,
+    ag_s, ag_r, own_s, w_s, misc_s, meta_s, meta_r, core_s, core_r, z_s, z_r,
+    inc_s, inc_r, ps_s, ps_r, r2_s, r2_r, r3_s, r3_r, r4_s, r4_r,
 ):
     n_exp, slots, width_ff = hid_hbm.shape
     cap = slots // NE
@@ -135,12 +135,15 @@
             sent, land = OWN.at[t], (ZC.at[v] if k == 2 else ZD.at[v])
         return remote(sent, land, z_s.at[v, k], z_r.at[v, k], next_z if k in (0, 2) else prev_z)
 
-    def add_blocks(t, lo, others):
+    def add_blocks(t, lo, others, into=None):
         for e in range(lo, lo + 2):
             acc = OWN[t, e].astype(F32)
             for other in others(e):
                 acc += other.astype(F32)
-            OWN[t, e] = acc.astype(BF)
+            if into is None:
+                OWN[t, e] = acc.astype(BF)
+            else:
+                dw_out[e, into * LANE:(into + 1) * LANE, :] = acc.astype(BF)
 
     def core_wait(t, lo):
         for e in (lo, lo + 1):
@@ -174,18 +177,12 @@
             add_blocks(t, 2, lambda e: [CR[t, e], ZB[v, e - 2]])
             z_hop(v, 3).start()
 
-    def dw_copy(v):
-        return pltpu.make_async_copy(
-            OWN.at[6 + v], dw_out.at[:, pl.ds(v * LANE, LANE), :], out_s.at[2 + v]
-        )
-
     def finish_down(v):
         z_hop(v, 2).wait_recv()
         z_hop(v, 3).wait_recv()
         for lo in (0, 2):
             core_wait(6 + v, lo)
-            add_blocks(6 + v, lo, lambda e: [CR[6 + v, e], ZC[v, e], ZD[v, e]])
-        dw_copy(v).start()
+            add_blocks(6 + v, lo, lambda e: [CR[6 + v, e], ZC[v, e], ZD[v, e]], into=v)
 
     comb_own = pltpu.make_async_copy(comb_hbm, META.at[me, pl.ds(0, 8)], misc_s.at[0])
     route_own = pltpu.make_async_copy(route_hbm, ROUTE, misc_s.at[4])
@@ -197,20 +194,20 @@
     hid_copy = pltpu.make_async_copy(hid_hbm, H, misc_s.at[1])
     in_copy = pltpu.make_async_copy(in_hbm, INP, misc_s.at[2])
     rw_copy = pltpu.make_async_copy(rw_hbm, RW, misc_s.at[3])
+    inc_own = pltpu.make_async_copy(
+        in_hbm.at[:, pl.ds(pl.multiple_of(me * LANE, LANE), LANE)], INC.at[me], misc_s.at[5]
+    )
 
     barrier = pltpu.get_barrier_semaphore()
-    for d in range(1, NE):
+    @pl.loop(1, NE)
+    def _(d):
         pl.semaphore_signal(barrier, inc=1, device_id=expert_dev(lax.rem(me + d, NE)),
                             device_id_type=pl.DeviceIdType.MESH)
-    for d in range(1, NDP):
+    @pl.loop(1, NDP)
+    def _(d):
         pl.semaphore_signal(barrier, inc=1, device_id=dp_dev(lax.rem(dp + d, NDP)),
                             device_id_type=pl.DeviceIdType.MESH)
     hid_copy.start()
-    for t in range(TICKS):
-        for h in range(2):
-            w_copy(t, h).start()
-    in_copy.start()
-    rw_copy.start()
     comb_own.wait()
     route_own.wait()
     META[me, 8:16, :] = ROUTE[...].astype(F32)
@@ -229,11 +226,29 @@
         got = META.at[plane_from(d)]
         return remote(got, got, meta_s.at[d], meta_r.at[d], plane_to(d))
 
+    def inc_send(d):
+        cols = pl.ds(pl.multiple_of(lax.rem(me + d, NE) * LANE, LANE), LANE)
+        return remote(INP.at[:, cols], INC.at[me], inc_s.at[d], inc_r.at[d], plane_to(d))
+
+    def inc_recv(d):
+        got = INC.at[plane_from(d)]
+        return remote(got, got, inc_s.at[d], inc_r.at[d], plane_to(d))
+
+    def build_gates(src):
+        block = META[src]
+        expert_id = lax.broadcasted_iota(jnp.int32, (NE * n_exp, LANE), 0).astype(F32)
+        gate = jnp.zeros((NE * n_exp, LANE), F32)
+        for k in range(8):
+            gate += jnp.where(expert_id == block[8 + k:9 + k], block[k:k + 1], 0.0)
+        GATE[src] = gate
+
     def build_codes():
-        for d in range(1, NE):
+        @pl.loop(1, NE)
+        def _(d):
             meta_recv(d).wait_recv()
 
-        for p in range(NE // 2):
+        @pl.loop(0, NE // 2)
+        def _(p):
             marks, gains = [], []
             for s2 in range(2):
                 block = META[2 * p + s2]
@@ -242,8 +257,9 @@
                     hit = rt == (me * n_exp + e).astype(F32)
                     marks.append(jnp.sum(jnp.where(hit, 1.0, 0.0), axis=0, keepdims=True))
                     gains.append(jnp.sum(jnp.where(hit, cb, 0.0), axis=0, keepdims=True))
-            CODES[8 * p:8 * p + 8, :] = jnp.concatenate(marks, axis=0)
-            GROW[8 * p:8 * p + 8, :] = jnp.concatenate(gains, axis=0)
+            at = pl.ds(pl.multiple_of(8 * p, 8), 8)
+            CODES[at, :] = jnp.concatenate(marks, axis=0)
+            GROW[at, :] = jnp.concatenate(gains, axis=0)
 
         marks = CODES[...]
         r = lax.broadcasted_iota(jnp.int32, (LANE, LANE), 0)
@@ -254,9 +270,11 @@
 
     def build_dispatch():
         place = lax.broadcasted_iota(jnp.int32, (pair, LANE), 0).astype(F32)
-        for p in range(NE // 2):
-            codes = CODES[8 * p:8 * p + 8, :]
-            gains = GROW[8 * p:8 * p + 8, :]
+        @pl.loop(0, NE // 2)
+        def _(p):
+            at = pl.ds(pl.multiple_of(8 * p, 8), 8)
+            codes = CODES[at, :]
+            gains = GROW[at, :]
             for e in range(n_exp):
                 first = jnp.where(place == codes[e:e + 1], 1.0, 0.0)
                 second = jnp.where(place - cap == codes[n_exp + e:n_exp + e + 1], 1.0, 0.0)
@@ -332,15 +350,29 @@
         def _():
             phase_start(t + 7, 0)
 
+        @pl.when(t + 2 == TICKS)
+        def _():
+            in_copy.wait()
+            @pl.loop(1, NE)
+            def _(d):
+                inc_send(d).start()
+
     phase_start(0, 0)
     phase_start(1, 0)
-    for d in range(1, NE):
+    @pl.loop(1, NE)
+    def _(d):
         meta_send(d).start()
     phase_wait(0, 0)
     phase_start(0, 1)
     phase_start(2, 0)
     phase_wait(0, 1)
     phase_start(0, 2)
+    for t in range(TICKS):
+        for h in range(2):
+            w_copy(t, h).start()
+    in_copy.start()
+    rw_copy.start()
+    inc_own.start()
     phase_wait(1, 0)
     phase_start(1, 1)
     phase_start(3, 0)
@@ -373,152 +405,34 @@
         def _():
             pair_up(t)
 
+        build_gates(2 * t)
+        build_gates(2 * t + 1)
+
     for e in range(n_exp):
         hg = HG[e]
-        for q in range(3):
-            W[e, q // 2, q % 2] = hg[q * LANE:(q + 1) * LANE].astype(BF)
+        hg_out[e] = hg.astype(BF)
         prod = jnp.sum(H[e].astype(F32) * hg, axis=1, keepdims=True)
         for p in range(NE // 2):
             row = jnp.sum(
                 S[p, e * pair:(e + 1) * pair, :].astype(F32) * prod[p * pair:(p + 1) * pair],
                 axis=0, keepdims=True,
             )
-            RR[p, e:e + 1, :] = row
-            RR[p, n_exp + e:n_exp + e + 1, :] = row
-    half = lax.broadcasted_iota(jnp.int32, (8, LANE), 0) // n_exp
-    mine = half == lax.rem(me, 2)
-    for p in range(NE // 2):
-        for s2 in range(2):
-            RSEND[2 * p + s2] = jnp.where(mine, RR[p, :, s2 * LANE:(s2 + 1) * LANE], 0.0)
-
-    def ret_send(d):
-        out = RSEND.at[lax.rem(me + d, NE)]
-        return remote(out, RRECV.at[me], ret_s.at[d], ret_r.at[d], plane_to(d))
-
-    def ret_recv(d):
-        got = RRECV.at[plane_from(d)]
-        return remote(got, got, ret_s.at[d], ret_r.at[d], plane_to(d))
-
-    for d in range(1, NE):
-        ret_send(d).start()
-    RRECV[me] = RSEND[me]
-
-    def hg_copy(e, q):
-        return pltpu.make_async_copy(
-            W.at[e, q // 2, q % 2], hg_out.at[e, pl.ds(q * LANE, LANE)], hg_s.at[e, q]
-        )
-
-    for e in range(n_exp):
-        for q in range(3):
-            hg_copy(e, q).start()
-
-    own_meta = META[me]
-    expert_id = lax.broadcasted_iota(jnp.int32, (NE * n_exp, LANE), 0).astype(F32)
-    gate = jnp.zeros((NE * n_exp, LANE), F32)
-    named = jnp.zeros((NE * n_exp, LANE), F32)
-    for k in range(8):
-        hit = expert_id == own_meta[8 + k:9 + k]
-        gate += jnp.where(hit, own_meta[k:k + 1], 0.0)
-        named += jnp.where(hit, 1.0, 0.0)
-
-    in_copy.wait()
+            at = n_exp * (p // 2) + e
+            PROD[at:at + 1, (p % 2) * 256:(p % 2) * 256 + 256] = row
+    PSB[me] = PROD[...].astype(BF)
+
+    def ps_send(d):
+        return remote(PSB.at[me], PSB.at[me], ps_s.at[d], ps_r.at[d], plane_to(d))
+
+    def ps_recv(d):
+        got = PSB.at[plane_from(d)]
+        return remote(got, got, ps_s.at[d], ps_r.at[d], plane_to(d))
+
+    @pl.loop(1, NE)
+    def _(d):
+        ps_send(d).start()
+    inc_own.wait()
     rw_copy.wait()
-    for d in range(1, NE):
-        ret_recv(d).wait_recv()
-    sums = jnp.concatenate([RRECV[2 * q] + RRECV[2 * q + 1] for q in range(NE // 2)], axis=0)
-    total = jnp.sum(sums, axis=0, keepdims=True)
-    dense = jnp.where(named > 0.5, sums - gate * total, 0.0).astype(BF)
-    rows_half = NE * n_exp // 2
-    for q in range(4):
-        cols = slice(q * 512, (q + 1) * 512)
-        part = jnp.dot(dense, INP[:, cols], preferred_element_type=F32)
-        for j in range(4):
-            block = part[:, j * LANE:(j + 1) * LANE]
-            RP[4 * q + j, 0] = block[:rows_half]
-            RP[4 * q + j, 1] = block[rows_half:]
-
-    other = dp_dev(2 * z + 1 - c)
-
-    def rc_send():
-        return remote(RP.at[:, 1 - c], RC, rc_s.at[0], rc_r.at[0], other)
-
-    def r1_send(d):
-        out = RP.at[lax.rem(me + d, NE), c]
-        return remote(out, R1.at[me], r1_s.at[d], r1_r.at[d], plane_to(d))
-
-    def r1_recv(d):
-        got = R1.at[plane_from(d)]
-        return remote(got, got, r1_s.at[d], r1_r.at[d], plane_to(d))
-
-    def r2_send(d):
-        to = dp_dev(2 * lax.rem(z + d, NZ) + c)
-        return remote(R2.at[z], R2.at[z], r2_s.at[d], r2_r.at[d], to)
-
-    def r2_recv(d):
-        got = R2.at[lax.rem(z + NZ - d, NZ)]
-        return remote(got, got, r2_s.at[d], r2_r.at[d], dp_dev(2 * lax.rem(z + d, NZ) + c))
-
-    def r3_send(d):
-        return remote(OUT.at[me, c], OUT.at[me, c], r3_s.at[d], r3_r.at[d], plane_to(d))
-
-    def r3_recv(d):
-        got = OUT.at[plane_from(d), c]
-        return remote(got, got, r3_s.at[d], r3_r.at[d], plane_to(d))
-
-    def r4_send():
-        return remote(OUT.at[:, c], OUT.at[:, c], rc_s.at[1], rc_r.at[1], other)
-
-    def r4_recv():
-        return remote(OUT.at[:, 1 - c], OUT.at[:, 1 - c], rc_s.at[1], rc_r.at[1], other)
-
-    rc_send().start()
-    rc_send().wait_recv()
-    for j in range(NE):
-        RP[j, c] += RC[j]
-    for d in range(1, NE):
-        r1_send(d).start()
-    R1[me] = RP[me, c]
-    for q in range(4):
-        cols = slice(q * 512, (q + 1) * 512)
-        IG[:, cols] = lax.dot_general(
-            dense, RW[:, cols], (((0,), (0,)), ((), ())), preferred_element_type=F32
-        ).astype(BF)
-    ig_copy = pltpu.make_async_copy(IG, ig_out, out_s.at[0])
-    ig_copy.start()
-
-    for d in range(1, NE):
-        r1_recv(d).wait_recv()
-    acc = R1[0]
-    for j in range(1, NE):
-        acc += R1[j]
-    R2[z] = acc
-    for d in range(1, NZ):
-        r2_send(d).start()
-    finish_down(0)
-    for d in range(1, NZ):
-        r2_recv(d).wait_recv()
-    acc = R2[0]
-    for j in range(1, NZ):
-        acc += R2[j]
-    OUT[me, c] = acc
-    for d in range(1, NE):
-        r3_send(d).start()
-    finish_down(1)
-    for d in range(1, NE):
-        r3_recv(d).wait_recv()
-    r4_send().start()
-    r4_recv().wait_recv()
-
-    def rp_copy(j, half):
-        return pltpu.make_async_copy(
-            OUT.at[j, half],
-            rp_out.at[pl.ds(half * rows_half, rows_half), pl.ds(j * LANE, LANE)],
-            rp_s.at[j, half],
-        )
-
-    for j in range(NE):
-        rp_copy(j, 0).start()
-        rp_copy(j, 1).start()
 
     @pl.loop(0, TICKS)
     def _(t):
@@ -526,29 +440,112 @@
             for k in range(8):
                 hop_drain(t, h, k)
 
-    for d in range(1, NE):
+    @pl.loop(1, NE)
+    def _(d):
+        inc_recv(d).wait_recv()
+    @pl.loop(1, NE)
+    def _(d):
+        ps_recv(d).wait_recv()
+
+    for i in range(NE // 2):
+        low, high = PSB[2 * i].astype(F32), PSB[2 * i + 1].astype(F32)
+        for g in range(4):
+            rows = slice(n_exp * g, n_exp * (g + 1))
+            SUMS[8 * i:8 * i + 8, g * 512:(g + 1) * 512] = jnp.concatenate(
+                [low[rows], high[rows]], axis=0
+            )
+    acc = jnp.zeros((NE * n_exp, LANE), F32)
+    for q in range(NE // 2):
+        both = []
+        for src in (2 * q, 2 * q + 1):
+            sums = SUMS[:, src * LANE:(src + 1) * LANE]
+            total = jnp.sum(sums, axis=0, keepdims=True)
+            dense = (sums - GATE[src] * total).astype(BF)
+            DENSE[src] = dense
+            both.append(dense)
+        acc += jnp.dot(
+            jnp.concatenate(both, axis=1), INC[2 * q:2 * q + 2].reshape(2 * LANE, LANE),
+            preferred_element_type=F32,
+        )
+    rows_half = NE * n_exp // 2
+    PF[0] = acc[:rows_half]
+    PF[1] = acc[rows_half:]
+
+    other = dp_dev(2 * z + 1 - c)
+
+    def r2_send(d):
+        to = lax.rem(dp + d, NDP)
+        return remote(PF.at[lax.rem(to, 2)], R2.at[dp], r2_s.at[d], r2_r.at[d], dp_dev(to))
+
+    def r2_recv(d):
+        got = R2.at[lax.rem(dp + NDP - d, NDP)]
+        return remote(got, got, r2_s.at[d], r2_r.at[d], dp_dev(lax.rem(dp + d, NDP)))
+
+    def r3_send(d):
+        return remote(OUT.at[c, me], OUT.at[c, me], r3_s.at[d], r3_r.at[d], plane_to(d))
+
+    def r3_recv(d):
+        got = OUT.at[c, plane_from(d)]
+        return remote(got, got, r3_s.at[d], r3_r.at[d], plane_to(d))
+
+    def r4_send():
+        return remote(OUT.at[c], OUT.at[c], r4_s, r4_r, other)
+
+    def r4_recv():
+        return remote(OUT.at[1 - c], OUT.at[1 - c], r4_s, r4_r, other)
+
+    @pl.loop(1, NDP)
+    def _(d):
+        r2_send(d).start()
+    R2[dp] = PF[c]
+    own_dense = DENSE[me]
+    for q in range(4):
+        cols = slice(q * 512, (q + 1) * 512)
+        ig_out[:, cols] = lax.dot_general(
+            own_dense, RW[:, cols], (((0,), (0,)), ((), ())), preferred_element_type=F32
+        ).astype(BF)
+    @pl.loop(1, NDP)
+    def _(d):
+        r2_recv(d).wait_recv()
+    acc = R2[0]
+    for j in range(1, NDP):
+        acc += R2[j]
+    OUT[c, me] = acc
+    @pl.loop(1, NE)
+    def _(d):
+        r3_send(d).start()
+    finish_down(0)
+    @pl.loop(1, NE)
+    def _(d):
         meta_send(d).wait_send()
-        ret_send(d).wait_send()
-        r1_send(d).wait_send()
-        r3_send(d).wait_send()
-    for d in range(1, NZ):
+        inc_send(d).wait_send()
+        ps_send(d).wait_send()
+    @pl.loop(1, NDP)
+    def _(d):
         r2_send(d).wait_send()
-    rc_send().wait_send()
-    r4_send().wait_send()
     for e in range(n_exp):
         core_hop(TICKS - 2, e).wait_send()
         core_hop(TICKS - 1, e).wait_send()
-    for v in range(2):
-        for k in range(4):
-            z_hop(v, k).wait_send()
-        dw_copy(v).wait()
-    for e in range(n_exp):
-        for q in range(3):
-            hg_copy(e, q).wait()
-    ig_copy.wait()
+    for k in range(4):
+        z_hop(0, k).wait_send()
+    for k in range(2):
+        z_hop(1, k).wait_send()
+    @pl.loop(1, NE)
+    def _(d):
+        r3_recv(d).wait_recv()
+    r4_send().start()
+    finish_down(1)
+    @pl.loop(1, NE)
+    def _(d):
+        r3_send(d).wait_send()
+    r4_recv().wait_recv()
     for j in range(NE):
-        rp_copy(j, 0).wait()
-        rp_copy(j, 1).wait()
+        for half in range(2):
+            rp_out[half * rows_half:(half + 1) * rows_half, j * LANE:(j + 1) * LANE] = OUT[half, j]
+
+    r4_send().wait_send()
+    for k in (2, 3):
+        z_hop(1, k).wait_send()
 
 
 def local(inputs, out_grad, combine, routes, saved_hidden, down_weight, router_weight):
@@ -581,9 +578,6 @@
             pltpu.VMEM((8, LANE), jnp.int32),
             pltpu.VMEM((NE * n_exp, LANE), F32),
             pltpu.VMEM((NE * n_exp, LANE), F32),
-            pltpu.VMEM((NE // 2, 8, 2 * LANE), F32),
-            pltpu.VMEM((NE, 8, LANE), F32),
-            pltpu.VMEM((NE, 8, LANE), F32),
             pltpu.VMEM((2, n_exp, LANE, ff), BF),
             pltpu.VMEM((TICKS, n_exp, LANE, ff), BF),
             pltpu.VMEM((TICKS, n_exp, LANE, ff), BF),
@@ -592,22 +586,21 @@
             pltpu.VMEM((2, n_exp, LANE, ff), BF),
             pltpu.VMEM((2, n_exp, LANE, ff), BF),
             pltpu.VMEM((tokens, width), BF),
+            pltpu.VMEM((NE, tokens, LANE), BF),
             pltpu.VMEM((total, width), BF),
-            pltpu.VMEM((tokens, width), BF),
-            pltpu.VMEM((NE, 2, total // 2, LANE), F32),
-            pltpu.VMEM((NE, total // 2, LANE), F32),
-            pltpu.VMEM((NE, total // 2, LANE), F32),
-            pltpu.VMEM((NZ, total // 2, LANE), F32),
-            pltpu.VMEM((NE, 2, total // 2, LANE), F32),
+            pltpu.VMEM((NE, total, LANE), F32),
+            pltpu.VMEM((16, 512), F32),
+            pltpu.VMEM((NE, 16, 512), BF),
+            pltpu.VMEM((total, NE * tokens), F32),
+            pltpu.VMEM((NE, total, LANE), BF),
+            pltpu.VMEM((2, total // 2, LANE), F32),
+            pltpu.VMEM((NDP, total // 2, LANE), F32),
+            pltpu.VMEM((2, NE, total // 2, LANE), F32),
             dma((TICKS, 2, 8)),
             dma((TICKS, 2, 8)),
             dma((TICKS, 2)),
             dma((TICKS, 2)),
-            dma((5,)),
-            dma((n_exp, 3)),
-            dma((4,)),
-            dma((NE,)),
-            dma((NE,)),
+            dma((6,)),
             dma((NE,)),
             dma((NE,)),
             dma((TICKS, n_exp)),
@@ -616,13 +609,14 @@
             dma((2, 4)),
             dma((NE,)),
             dma((NE,)),
-            dma((NZ,)),
-            dma((NZ,)),
-            dma((NE,)),
-            dma((NE,)),
-            dma((2,)),
-            dma((2,)),
-            dma((NE, 2)),
+            dma((NE,)),
+            dma((NE,)),
+            dma((NDP,)),
+            dma((NDP,)),
+            dma((NE,)),
+            dma((NE,)),
+            dma,
+            dma,
         ],
         compiler_params=pltpu.CompilerParams(
             collective_id=0, has_side_effects=True, vmem_limit_bytes=58 * 2**20

time: 103 us -> 103 us (level)
  no operation moved by 1% of the time
where the time goes in v4:
time: 103 us
  Pallas kernels  98.1 us (95%)
  local copies, waits for them, and re-layouts  4.14 us (4%)
    pallas_call x1, Pallas kernels, local(): pl.pallas_call(fused, out_shape=(pltpu.VMEM((n_exp, slots, ff), BF), pltp...  98.1 us
    unnamed x4, local copies, waits for them, and re-layouts  4.14 us

profile of v4, /device:TPU:1, one launch (start us, length us, event | category | flops | bytes accessed | tf_op | source)
XLA Modules:
  0.0 102.9 jit_solution(12656786931055130974)
XLA Ops:
  0.6 98.1 %moe_down_backward.1 = (bf16[4,384,768]{2,1,0:T(8,128)(2,1)S(1)}, bf16[4,256,768]{2,1,0:T(8,128)(2,1)S(1)}, bf16[128,2048]{1,0:T(8,128)(2,1)S(1)}, f32[64,2048]{1,0:T(8,128)S(1)}) custom-call(f32[8,128]{1,0:T(8,128)} %bitcast.6, s32[8,128]{1,0:T(8,128)} %bitcast.7, bf16[128,2048]{1,0:T(8,128)(2,1)} %og_hbm.1, bf16[4,384,768]{2,1,0:T(8,128)(2,1)} %bitcast.5, ...), custom_call_target="tpu_custom_call" | custom-call | tf_op jit(solution)/shard_map/moe_down_backward/pallas_call | solution.py:559
  98.7 1.4 %copy.15 = bf16[1,4,16,24,768]{4,3,2,1,0:T(8,128)(2,1)} copy(bf16[1,4,16,24,768]{4,3,2,1,0:T(8,128)(2,1)S(1)} %bitcast.4) | data formatting | bytes 4718592
  100.1 0.8 copy.17
  100.9 0.8 copy.18
  101.7 1.1 %copy.16 = bf16[4,256,768]{2,1,0:T(8,128)(2,1)} copy(bf16[4,256,768]{2,1,0:T(8,128)(2,1)S(1)} %get-tuple-element.13) | data formatting | bytes 3145728

commit v5 on v3

--- a/solution.py
+++ b/solution.py
@@ -206,11 +206,6 @@
         pl.semaphore_signal(barrier, inc=1, device_id=dp_dev(lax.rem(dp + d, NDP)),
                             device_id_type=pl.DeviceIdType.MESH)
     hid_copy.start()
-    for t in range(TICKS):
-        for h in range(2):
-            w_copy(t, h).start()
-    in_copy.start()
-    rw_copy.start()
     comb_own.wait()
     route_own.wait()
     META[me, 8:16, :] = ROUTE[...].astype(F32)
@@ -341,6 +336,11 @@
     phase_start(2, 0)
     phase_wait(0, 1)
     phase_start(0, 2)
+    for t in range(TICKS):
+        for h in range(2):
+            w_copy(t, h).start()
+    in_copy.start()
+    rw_copy.start()
     phase_wait(1, 0)
     phase_start(1, 1)
     phase_start(3, 0)
@@ -423,6 +423,12 @@
 
     in_copy.wait()
     rw_copy.wait()
+    @pl.loop(0, TICKS)
+    def _(t):
+        for h in range(2):
+            for k in range(8):
+                hop_drain(t, h, k)
+
     for d in range(1, NE):
         ret_recv(d).wait_recv()
     sums = jnp.concatenate([RRECV[2 * q] + RRECV[2 * q + 1] for q in range(NE // 2)], axis=0)
@@ -519,12 +525,6 @@
     for j in range(NE):
         rp_copy(j, 0).start()
         rp_copy(j, 1).start()
-
-    @pl.loop(0, TICKS)
-    def _(t):
-        for h in range(2):
-            for k in range(8):
-                hop_drain(t, h, k)
 
     for d in range(1, NE):
         meta_send(d).wait_send()

time: 103 us -> 103 us (level)
  no operation moved by 1% of the time
where the time goes in v5:
time: 103 us
  Pallas kernels  98 us (95%)
  local copies, waits for them, and re-layouts  4.14 us (4%)
    pallas_call x1, Pallas kernels, local(): pl.pallas_call(fused, out_shape=(pltpu.VMEM((n_exp, slots, ff), BF), pltp...  98 us
    unnamed x4, local copies, waits for them, and re-layouts  4.14 us

profile of v5, /device:TPU:1, one launch (start us, length us, event | category | flops | bytes accessed | tf_op | source)
XLA Modules:
  0.0 102.8 jit_solution(4620084074495198946)
XLA Ops:
  0.6 98.0 %moe_down_backward.1 = (bf16[4,384,768]{2,1,0:T(8,128)(2,1)S(1)}, bf16[4,256,768]{2,1,0:T(8,128)(2,1)S(1)}, bf16[128,2048]{1,0:T(8,128)(2,1)S(1)}, f32[64,2048]{1,0:T(8,128)S(1)}) custom-call(f32[8,128]{1,0:T(8,128)} %bitcast.6, s32[8,128]{1,0:T(8,128)} %bitcast.7, bf16[128,2048]{1,0:T(8,128)(2,1)} %og_hbm.1, bf16[4,384,768]{2,1,0:T(8,128)(2,1)} %bitcast.5, ...), custom_call_target="tpu_custom_call" | custom-call | tf_op jit(solution)/shard_map/moe_down_backward/pallas_call | solution.py:562
  98.7 1.4 %copy.15 = bf16[1,4,16,24,768]{4,3,2,1,0:T(8,128)(2,1)} copy(bf16[1,4,16,24,768]{4,3,2,1,0:T(8,128)(2,1)S(1)} %bitcast.4) | data formatting | bytes 4718592
  100.1 0.8 copy.17
  100.9 0.8 copy.18
  101.7 1.1 %copy.16 = bf16[4,256,768]{2,1,0:T(8,128)(2,1)} copy(bf16[4,256,768]{2,1,0:T(8,128)(2,1)S(1)} %get-tuple-element.13) | data formatting | bytes 3145728
